TPU v7x, 512 devices: a whole 4x4x16 slice. The times are simulated.
512 devices in a mesh: space: 128 (over z, y, x_lo), shot: 4 (over x_hi, core).
Axes of the slice: x: 4 (x_hi: 2, x_lo: 2; x = x_hi * 2 + x_lo), y: 4, z: 16, core: 2. Of those that a mesh axis runs over, the one named last changes fastest.
Arguments:
- velocity: float32 [1024, 192, 128], P('space'), may hold values from 1.5 to 4.5
- wave_now: float32 [4, 1024, 192, 128], P('shot', 'space'), may hold values from -6 to 6
- wave_prev: float32 [4, 1024, 192, 128], P('shot', 'space'), may hold values from -6 to 6
- adjoint_now: float32 [4, 1024, 192, 128], P('shot', 'space'), may hold values from -6 to 6
- adjoint_prev: float32 [4, 1024, 192, 128], P('shot', 'space'), may hold values from -6 to 6
- source_cells: int32 [4, 128], P('shot'), may hold values from 0 to 25165823, as said below
- wavelet: float32 [4, 10, 128], P('shot'), may hold values from -24 to 24
- receiver_cells: int32 [65536], P('space'), may hold values from 0 to 196607, as said below
- receiver_counts: int32 [128], P('space'), may hold values from 128 to 512, as said below
- observed: float32 [4, 10, 65536], P('shot', None, 'space'), may hold values from -24 to 24
Outputs:
- gradient: float32 [1024, 192, 128], P('space', 'shot')
Inputs may be any that keep to these rules, and one draw needn't show every extreme that they name: `source_cells`: flat indices into the whole grid (first dimension slowest); the 128 cells of one shot group are distinct. `receiver_cells`: flat indices within one device's block of 8 x 192 x 128 cells (first dimension slowest); the 512 cells of one block are distinct. `receiver_counts`: the live slots of a block come first.
All inputs are finite; a program needn't handle non-finite values.
Results may differ from a plain program's by a relative error of at most 0.00002.
Values sent between devices are 32-bit elements; how exact they have to be, the bound alone decides.
No kernel may reach another device: no remote copies, remote signals or barrier semaphores. Data moves between devices by JAX's collectives and lax.ppermute only.
A program may use at most 64 MiB of HBM per device.

v0:
```python
import jax
import jax.numpy as jnp
from jax import lax
from jax.sharding import PartitionSpec as P

TAPS = (-205.0 / 72.0, 8.0 / 5.0, -1.0 / 5.0, 8.0 / 315.0, -1.0 / 560.0)
COURANT = 0.09


def with_halo(block, sides, width):
    for axis, dim in sides:
        count = lax.axis_size(axis)
        forward = [(i, i + 1) for i in range(count - 1)]
        backward = [(target, source) for source, target in forward]
        low = lax.ppermute(
            lax.slice_in_dim(block, block.shape[dim] - width, None, axis=dim), axis, forward
        )
        high = lax.ppermute(lax.slice_in_dim(block, 0, width, axis=dim), axis, backward)
        block = jnp.concatenate([low, block, high], axis=dim)
    return block


def laplace(widened):
    length_x = widened.shape[0] - 8
    extent_y = widened.shape[1]
    extent_z = widened.shape[2]
    padded = jnp.pad(widened, ((0, 0), (4, 4), (4, 4)))
    centre = widened[4 : 4 + length_x]
    result = 3.0 * TAPS[0] * centre
    for distance in range(1, 5):
        beside_all = (
            padded[4 + distance : 4 + distance + length_x, 4 : 4 + extent_y, 4 : 4 + extent_z]
            + padded[4 - distance : 4 - distance + length_x, 4 : 4 + extent_y, 4 : 4 + extent_z]
        )
        beside_all = (
            beside_all
            + padded[4 : 4 + length_x, 4 + distance : 4 + distance + extent_y, 4 : 4 + extent_z]
            + padded[4 : 4 + length_x, 4 - distance : 4 - distance + extent_y, 4 : 4 + extent_z]
        )
        beside_all = (
            beside_all
            + padded[4 : 4 + length_x, 4 : 4 + extent_y, 4 + distance : 4 + distance + extent_z]
            + padded[4 : 4 + length_x, 4 : 4 + extent_y, 4 - distance : 4 - distance + extent_z]
        )
        result = result + TAPS[distance] * beside_all
    return result


def edge_layers(field):
    return with_halo(field, (("space", 0),), 4)


def add_at(field, target, amounts):
    size_all = field.size
    inside = (target >= 0) & (target < size_all)
    flat_field = (
        field.reshape(-1).at[jnp.where(inside, target, 0)].add(jnp.where(inside, amounts, 0.0))
    )
    return flat_field.reshape(field.shape)


def per_device(
    velocity,
    wave_now,
    wave_prev,
    adjoint_now,
    adjoint_prev,
    source_cells,
    wavelet,
    receiver_cells,
    receiver_counts,
    observed,
):
    extent_x, extent_y, extent_z = velocity.shape
    plane_cells = extent_y * extent_z
    courant_sq = (COURANT * velocity) ** 2
    position = lax.axis_index("space")
    local_sources = source_cells[0] - position * (extent_x * plane_cells)
    pulses = wavelet[0]

    def forward(carried, source_pulse):
        current, former = carried
        latest = 2.0 * current - former + courant_sq * laplace(edge_layers(current))
        latest = add_at(latest, local_sources, source_pulse)
        acceleration = latest - 2.0 * current + former
        return ((latest, current), (acceleration, latest.reshape(-1)[receiver_cells]))

    _, (accelerations, traces) = lax.scan(forward, (wave_now[0], wave_prev[0]), pulses)
    live_slots = (jnp.arange(receiver_cells.shape[0], dtype=jnp.int32) < receiver_counts[0]).astype(
        jnp.float32
    )
    misfit = (traces - observed[0]) * live_slots

    def backward(carried, inputs):
        following, furthest, imaging = carried
        acceleration, residual = inputs
        earlier = 2.0 * following - furthest + courant_sq * laplace(edge_layers(following))
        earlier = earlier.reshape(-1).at[receiver_cells].add(residual).reshape(velocity.shape)
        return ((earlier, following, imaging + earlier * acceleration), None)

    empty_field = jnp.zeros_like(velocity)
    (_, _, imaging), _ = lax.scan(
        backward,
        (adjoint_now[0], adjoint_prev[0], empty_field),
        (accelerations, misfit),
        reverse=True,
    )
    band_rows = extent_y // lax.axis_size("shot")
    offset = lax.axis_index("shot") * band_rows
    factor = lax.dynamic_slice_in_dim(-2.0 / velocity**3, offset, band_rows, 1)
    summed = lax.psum(imaging, "shot")
    own_band = lax.dynamic_slice_in_dim(summed, offset, band_rows, 1)
    return factor * own_band


def solution(mesh):
    in_specs = (
        P("space", None, None),
        P("shot", "space", None, None),
        P("shot", "space", None, None),
        P("shot", "space", None, None),
        P("shot", "space", None, None),
        P("shot", None),
        P("shot", None, None),
        P("space"),
        P("space"),
        P("shot", None, "space"),
    )
    out_specs = P("space", "shot", None)
    return jax.shard_map(
        per_device, mesh=mesh, in_specs=in_specs, out_specs=out_specs, check_vma=False
    )
```

profile of v0, /device:TPU:1, one launch (start us, length us, event | category | flops | bytes accessed | tf_op | source)
XLA Modules:
  0.0 773.1 jit_solution(16620281286347901368)
XLA Ops:
  12.2 333.3 %while.37 = (s32[]{:T(128)}, f32[8,192,128]{2,1,0:T(8,128)S(1)}, f32[8,192,128]{2,1,0:T(8,128)}, f32[10,8,192,128]{3,2,1,0:T(8,128)}, f32[10,512]{1,0:T(8,128)},...) while((s32[]{:T(128)}, f32[8,192,128]{2,1,0:T(8,128)S(1)}, ...), condition=%wide.region_2.3_spmd, body=%wide.region_0.2_spmd.sunk | while | flops 13609986 | bytes 43449096 | solution.py:88
  13.0 4.0 collective-permute-start.1
  22.2 13.2 %collective-permute-done = f32[4,192,128]{2,1,0:T(8,128)S(1)} collective-permute-done((f32[4,192,128]{2,1,0:T(8,128)S(1)}, f32[4,192,128]{2,1,0:T(8,128)S(1)}, u32[]{:S(2)}, u32[]{:S(2)}) %collective-permute-start) | collective-permute-done | bytes 393248 | tf_op jit(solution)/shard_map/while/body/eval_jaxpr/ppermute | solution.py:18
  56.1 4.0 collective-permute-done.1
  60.3 10.1 %collective-permute-done = f32[4,192,128]{2,1,0:T(8,128)S(1)} collective-permute-done((f32[4,192,128]{2,1,0:T(8,128)S(1)}, f32[4,192,128]{2,1,0:T(8,128)S(1)}, u32[]{:S(2)}, u32[]{:S(2)}) %collective-permute-start) | collective-permute-done | bytes 393248 | tf_op jit(solution)/shard_map/while/body/eval_jaxpr/ppermute | solution.py:18
  94.5 9.8 %collective-permute-done = f32[4,192,128]{2,1,0:T(8,128)S(1)} collective-permute-done((f32[4,192,128]{2,1,0:T(8,128)S(1)}, f32[4,192,128]{2,1,0:T(8,128)S(1)}, u32[]{:S(2)}, u32[]{:S(2)}) %collective-permute-start) | collective-permute-done | bytes 393248 | tf_op jit(solution)/shard_map/while/body/eval_jaxpr/ppermute | solution.py:18
  127.4 9.7 %collective-permute-done = f32[4,192,128]{2,1,0:T(8,128)S(1)} collective-permute-done((f32[4,192,128]{2,1,0:T(8,128)S(1)}, f32[4,192,128]{2,1,0:T(8,128)S(1)}, u32[]{:S(2)}, u32[]{:S(2)}) %collective-permute-start) | collective-permute-done | bytes 393248 | tf_op jit(solution)/shard_map/while/body/eval_jaxpr/ppermute | solution.py:18
  159.2 8.4 %collective-permute-done = f32[4,192,128]{2,1,0:T(8,128)S(1)} collective-permute-done((f32[4,192,128]{2,1,0:T(8,128)S(1)}, f32[4,192,128]{2,1,0:T(8,128)S(1)}, u32[]{:S(2)}, u32[]{:S(2)}) %collective-permute-start) | collective-permute-done | bytes 393248 | tf_op jit(solution)/shard_map/while/body/eval_jaxpr/ppermute | solution.py:18
  190.1 8.0 %collective-permute-done = f32[4,192,128]{2,1,0:T(8,128)S(1)} collective-permute-done((f32[4,192,128]{2,1,0:T(8,128)S(1)}, f32[4,192,128]{2,1,0:T(8,128)S(1)}, u32[]{:S(2)}, u32[]{:S(2)}) %collective-permute-start) | collective-permute-done | bytes 393248 | tf_op jit(solution)/shard_map/while/body/eval_jaxpr/ppermute | solution.py:18
  219.3 6.0 collective-permute-done
  245.8 4.1 collective-permute-done.1
  250.1 10.8 %collective-permute-done = f32[4,192,128]{2,1,0:T(8,128)S(1)} collective-permute-done((f32[4,192,128]{2,1,0:T(8,128)S(1)}, f32[4,192,128]{2,1,0:T(8,128)S(1)}, u32[]{:S(2)}, u32[]{:S(2)}) %collective-permute-start) | collective-permute-done | bytes 393248 | tf_op jit(solution)/shard_map/while/body/eval_jaxpr/ppermute | solution.py:18
  275.3 5.3 collective-permute-start.1
  285.8 11.1 %collective-permute-done = f32[4,192,128]{2,1,0:T(8,128)S(1)} collective-permute-done((f32[4,192,128]{2,1,0:T(8,128)S(1)}, f32[4,192,128]{2,1,0:T(8,128)S(1)}, u32[]{:S(2)}, u32[]{:S(2)}) %collective-permute-start) | collective-permute-done | bytes 393248 | tf_op jit(solution)/shard_map/while/body/eval_jaxpr/ppermute | solution.py:18
  311.3 5.3 collective-permute-start.1
  321.8 10.1 %collective-permute-done = f32[4,192,128]{2,1,0:T(8,128)S(1)} collective-permute-done((f32[4,192,128]{2,1,0:T(8,128)S(1)}, f32[4,192,128]{2,1,0:T(8,128)S(1)}, u32[]{:S(2)}, u32[]{:S(2)}) %collective-permute-start) | collective-permute-done | bytes 393248 | tf_op jit(solution)/shard_map/while/body/eval_jaxpr/ppermute | solution.py:18
  346.9 325.5 %while.38 = (s32[]{:T(128)}, f32[8,192,128]{2,1,0:T(8,128)S(1)}, f32[8,192,128]{2,1,0:T(8,128)}, f32[8,192,128]{2,1,0:T(8,128)}, f32[8,192,128]{2,1,0:T(8,128)S(...) while((s32[]{:T(128)}, f32[8,192,128]{2,1,0:T(8,128)S(1)}, ...), condition=%wide.region_5.6_spmd.clone, body=%wide.region_3.5_spmd.clone.sunk | while | flops 13607940 | bytes 49729836 | solution.py:102
  347.0 5.0 collective-permute-start.3
  357.0 6.4 collective-permute-done.2
  368.6 3.7 scatter_fusion.1
  375.1 5.3 collective-permute-start.3
  382.4 12.6 %collective-permute-done.3 = f32[4,192,128]{2,1,0:T(8,128)S(1)} collective-permute-done((f32[4,192,128]{2,1,0:T(8,128)S(1)}, f32[4,192,128]{2,1,0:T(8,128)S(1)}, u32[]{:S(2)}, u32[]{:S(2)}) %collective-permute-start.3) | collective-permute-done | bytes 393248 | tf_op jit(solution)/shard_map/while/body/eval_jaxpr/ppermute | solution.py:15
  395.2 5.2 collective-permute-done.2
  405.6 3.7 scatter_fusion.1
  412.1 5.3 collective-permute-start.3
  422.9 10.5 %collective-permute-done.2 = f32[4,192,128]{2,1,0:T(8,128)S(1)} collective-permute-done((f32[4,192,128]{2,1,0:T(8,128)S(1)}, f32[4,192,128]{2,1,0:T(8,128)S(1)}, u32[]{:S(2)}, u32[]{:S(2)}) %collective-permute-start.2) | collective-permute-done | bytes 393248 | tf_op jit(solution)/shard_map/while/body/eval_jaxpr/ppermute | solution.py:18
  438.6 3.7 scatter_fusion.1
  445.0 5.2 collective-permute-start.3
  452.3 5.2 collective-permute-done.3
  457.7 7.9 %collective-permute-done.2 = f32[4,192,128]{2,1,0:T(8,128)S(1)} collective-permute-done((f32[4,192,128]{2,1,0:T(8,128)S(1)}, f32[4,192,128]{2,1,0:T(8,128)S(1)}, u32[]{:S(2)}, u32[]{:S(2)}) %collective-permute-start.2) | collective-permute-done | bytes 393248 | tf_op jit(solution)/shard_map/while/body/eval_jaxpr/ppermute | solution.py:18
  470.8 3.7 scatter_fusion.1
  477.3 5.3 collective-permute-start.3
  484.7 5.8 collective-permute-done.3
  499.3 3.7 scatter_fusion.1
  505.8 4.7 collective-permute-start.3
  512.6 12.5 %collective-permute-done.3 = f32[4,192,128]{2,1,0:T(8,128)S(1)} collective-permute-done((f32[4,192,128]{2,1,0:T(8,128)S(1)}, f32[4,192,128]{2,1,0:T(8,128)S(1)}, u32[]{:S(2)}, u32[]{:S(2)}) %collective-permute-start.3) | collective-permute-done | bytes 393248 | tf_op jit(solution)/shard_map/while/body/eval_jaxpr/ppermute | solution.py:15
  525.2 5.5 collective-permute-done.2
  542.4 5.0 collective-permute-start.3
  553.0 10.7 %collective-permute-done.2 = f32[4,192,128]{2,1,0:T(8,128)S(1)} collective-permute-done((f32[4,192,128]{2,1,0:T(8,128)S(1)}, f32[4,192,128]{2,1,0:T(8,128)S(1)}, u32[]{:S(2)}, u32[]{:S(2)}) %collective-permute-start.2) | collective-permute-done | bytes 393248 | tf_op jit(solution)/shard_map/while/body/eval_jaxpr/ppermute | solution.py:18
  575.4 5.0 collective-permute-start.3
  582.4 5.3 collective-permute-done.3
  587.8 7.9 %collective-permute-done.2 = f32[4,192,128]{2,1,0:T(8,128)S(1)} collective-permute-done((f32[4,192,128]{2,1,0:T(8,128)S(1)}, f32[4,192,128]{2,1,0:T(8,128)S(1)}, u32[]{:S(2)}, u32[]{:S(2)}) %collective-permute-start.2) | collective-permute-done | bytes 393248 | tf_op jit(solution)/shard_map/while/body/eval_jaxpr/ppermute | solution.py:18
  607.4 5.3 collective-permute-start.3
  614.8 5.8 collective-permute-done.3
  635.9 4.7 collective-permute-start.3
  642.6 12.5 %collective-permute-done.3 = f32[4,192,128]{2,1,0:T(8,128)S(1)} collective-permute-done((f32[4,192,128]{2,1,0:T(8,128)S(1)}, f32[4,192,128]{2,1,0:T(8,128)S(1)}, u32[]{:S(2)}, u32[]{:S(2)}) %collective-permute-start.3) | collective-permute-done | bytes 393248 | tf_op jit(solution)/shard_map/while/body/eval_jaxpr/ppermute | solution.py:15
  655.4 5.5 collective-permute-done.2
  672.5 92.0 %all-reduce.4.cloned.1.call-done = f32[8,192,128]{2,1,0:T(8,128)} async-done(((f32[8,192,128]{2,1,0:T(8,128)}), f32[8,192,128]{2,1,0:T(8,128)}) %all-reduce.4.cloned.1.call-update) | async-done | bytes 786448 | tf_op jit(solution)/shard_map/psum | solution.py:111
  (442 shorter events, 356.1 us)
Async XLA Ops:
  6.5 758.0 %all-reduce.4.cloned.1.call-start = ((), (), s32[]{:S(2)}) async-start(), calls=%async_computation | async-start | bytes 1572864 | tf_op jit(solution)/shard_map/psum | solution.py:111
  12.2 334.7 %copy-start.1 = (f32[1,8,192,128]{3,2,1,0:T(8,128)S(1)}, f32[1,8,192,128]{3,2,1,0:T(8,128)}, u32[]{:S(2)}) copy-start(f32[1,8,192,128]{3,2,1,0:T(8,128)} %param.17) | copy-start | bytes 2359300
  13.0 9.0 %collective-permute-start.1 = (f32[4,192,128]{2,1,0:T(8,128)}, f32[4,192,128]{2,1,0:T(8,128)S(1)}, u32[]{:S(2)}, u32[]{:S(2)}) collective-permute-start(f32[4,192,128]{2,1,0:T(8,128)} %get-tuple-element.457), channel_id=1, source_target_pairs={{0,4},{4,8},{8,12},{12,16},{16,20},{20,24},{24,28},{28,32},{32,36}... | collective-permute-start | bytes 1179656 | tf_op jit(solution)/shard_map/while/body/eval_jaxpr/ppermute | solution.py:15
  17.0 18.4 %collective-permute-start = (f32[4,192,128]{2,1,0:T(8,128)S(1)}, f32[4,192,128]{2,1,0:T(8,128)S(1)}, u32[]{:S(2)}, u32[]{:S(2)}) collective-permute-start(f32[4,192,128]{2,1,0:T(8,128)S(1)} %get-tuple-element.456), channel_id=1, source_target_pairs={{4,0},{8,4},{12,8},{16,12},{20,16},{24,20},{28,24},{32,28},{36,32}... | collective-permute-start | bytes 1179656 | tf_op jit(solution)/shard_map/while/body/eval_jaxpr/ppermute | solution.py:18
  22.2 14.2 %copy-start.2 = (f32[8,192,128]{2,1,0:T(8,128)S(1)}, f32[8,192,128]{2,1,0:T(8,128)}, u32[]{:S(2)}) copy-start(f32[8,192,128]{2,1,0:T(8,128)} %get-tuple-element.485) | copy-start | bytes 2359300 | tf_op jit(solution)/shard_map/while
  49.9 10.3 %collective-permute-start.1 = (f32[4,192,128]{2,1,0:T(8,128)}, f32[4,192,128]{2,1,0:T(8,128)S(1)}, u32[]{:S(2)}, u32[]{:S(2)}) collective-permute-start(f32[4,192,128]{2,1,0:T(8,128)} %get-tuple-element.457), channel_id=1, source_target_pairs={{0,4},{4,8},{8,12},{12,16},{16,20},{20,24},{24,28},{28,32},{32,36}... | collective-permute-start | bytes 1179656 | tf_op jit(solution)/shard_map/while/body/eval_jaxpr/ppermute | solution.py:15
  53.0 17.5 %collective-permute-start = (f32[4,192,128]{2,1,0:T(8,128)S(1)}, f32[4,192,128]{2,1,0:T(8,128)S(1)}, u32[]{:S(2)}, u32[]{:S(2)}) collective-permute-start(f32[4,192,128]{2,1,0:T(8,128)S(1)} %get-tuple-element.456), channel_id=1, source_target_pairs={{4,0},{8,4},{12,8},{16,12},{20,16},{24,20},{28,24},{32,28},{36,32}... | collective-permute-start | bytes 1179656 | tf_op jit(solution)/shard_map/while/body/eval_jaxpr/ppermute | solution.py:18
  84.9 9.3 %collective-permute-start.1 = (f32[4,192,128]{2,1,0:T(8,128)}, f32[4,192,128]{2,1,0:T(8,128)S(1)}, u32[]{:S(2)}, u32[]{:S(2)}) collective-permute-start(f32[4,192,128]{2,1,0:T(8,128)} %get-tuple-element.457), channel_id=1, source_target_pairs={{0,4},{4,8},{8,12},{12,16},{16,20},{20,24},{24,28},{28,32},{32,36}... | collective-permute-start | bytes 1179656 | tf_op jit(solution)/shard_map/while/body/eval_jaxpr/ppermute | solution.py:15
  88.1 16.2 %collective-permute-start = (f32[4,192,128]{2,1,0:T(8,128)S(1)}, f32[4,192,128]{2,1,0:T(8,128)S(1)}, u32[]{:S(2)}, u32[]{:S(2)}) collective-permute-start(f32[4,192,128]{2,1,0:T(8,128)S(1)} %get-tuple-element.456), channel_id=1, source_target_pairs={{4,0},{8,4},{12,8},{16,12},{20,16},{24,20},{28,24},{32,28},{36,32}... | collective-permute-start | bytes 1179656 | tf_op jit(solution)/shard_map/while/body/eval_jaxpr/ppermute | solution.py:18
  118.8 8.4 %collective-permute-start.1 = (f32[4,192,128]{2,1,0:T(8,128)}, f32[4,192,128]{2,1,0:T(8,128)S(1)}, u32[]{:S(2)}, u32[]{:S(2)}) collective-permute-start(f32[4,192,128]{2,1,0:T(8,128)} %get-tuple-element.457), channel_id=1, source_target_pairs={{0,4},{4,8},{8,12},{12,16},{16,20},{20,24},{24,28},{28,32},{32,36}... | collective-permute-start | bytes 1179656 | tf_op jit(solution)/shard_map/while/body/eval_jaxpr/ppermute | solution.py:15
  121.9 15.2 %collective-permute-start = (f32[4,192,128]{2,1,0:T(8,128)S(1)}, f32[4,192,128]{2,1,0:T(8,128)S(1)}, u32[]{:S(2)}, u32[]{:S(2)}) collective-permute-start(f32[4,192,128]{2,1,0:T(8,128)S(1)} %get-tuple-element.456), channel_id=1, source_target_pairs={{4,0},{8,4},{12,8},{16,12},{20,16},{24,20},{28,24},{32,28},{36,32}... | collective-permute-start | bytes 1179656 | tf_op jit(solution)/shard_map/while/body/eval_jaxpr/ppermute | solution.py:18
  151.6 7.5 collective-permute-start.1
  154.0 13.6 %collective-permute-start = (f32[4,192,128]{2,1,0:T(8,128)S(1)}, f32[4,192,128]{2,1,0:T(8,128)S(1)}, u32[]{:S(2)}, u32[]{:S(2)}) collective-permute-start(f32[4,192,128]{2,1,0:T(8,128)S(1)} %get-tuple-element.456), channel_id=1, source_target_pairs={{4,0},{8,4},{12,8},{16,12},{20,16},{24,20},{28,24},{32,28},{36,32}... | collective-permute-start | bytes 1179656 | tf_op jit(solution)/shard_map/while/body/eval_jaxpr/ppermute | solution.py:18
  182.1 7.8 %collective-permute-start.1 = (f32[4,192,128]{2,1,0:T(8,128)}, f32[4,192,128]{2,1,0:T(8,128)S(1)}, u32[]{:S(2)}, u32[]{:S(2)}) collective-permute-start(f32[4,192,128]{2,1,0:T(8,128)} %get-tuple-element.457), channel_id=1, source_target_pairs={{0,4},{4,8},{8,12},{12,16},{16,20},{20,24},{24,28},{28,32},{32,36}... | collective-permute-start | bytes 1179656 | tf_op jit(solution)/shard_map/while/body/eval_jaxpr/ppermute | solution.py:15
  184.9 13.2 %collective-permute-start = (f32[4,192,128]{2,1,0:T(8,128)S(1)}, f32[4,192,128]{2,1,0:T(8,128)S(1)}, u32[]{:S(2)}, u32[]{:S(2)}) collective-permute-start(f32[4,192,128]{2,1,0:T(8,128)S(1)} %get-tuple-element.456), channel_id=1, source_target_pairs={{4,0},{8,4},{12,8},{16,12},{20,16},{24,20},{28,24},{32,28},{36,32}... | collective-permute-start | bytes 1179656 | tf_op jit(solution)/shard_map/while/body/eval_jaxpr/ppermute | solution.py:18
  212.6 6.5 collective-permute-start.1
  214.1 11.2 %collective-permute-start = (f32[4,192,128]{2,1,0:T(8,128)S(1)}, f32[4,192,128]{2,1,0:T(8,128)S(1)}, u32[]{:S(2)}, u32[]{:S(2)}) collective-permute-start(f32[4,192,128]{2,1,0:T(8,128)S(1)} %get-tuple-element.456), channel_id=1, source_target_pairs={{4,0},{8,4},{12,8},{16,12},{20,16},{24,20},{28,24},{32,28},{36,32}... | collective-permute-start | bytes 1179656 | tf_op jit(solution)/shard_map/while/body/eval_jaxpr/ppermute | solution.py:18
  239.7 10.2 %collective-permute-start.1 = (f32[4,192,128]{2,1,0:T(8,128)}, f32[4,192,128]{2,1,0:T(8,128)S(1)}, u32[]{:S(2)}, u32[]{:S(2)}) collective-permute-start(f32[4,192,128]{2,1,0:T(8,128)} %get-tuple-element.457), channel_id=1, source_target_pairs={{0,4},{4,8},{8,12},{12,16},{16,20},{20,24},{24,28},{28,32},{32,36}... | collective-permute-start | bytes 1179656 | tf_op jit(solution)/shard_map/while/body/eval_jaxpr/ppermute | solution.py:15
  242.6 18.3 %collective-permute-start = (f32[4,192,128]{2,1,0:T(8,128)S(1)}, f32[4,192,128]{2,1,0:T(8,128)S(1)}, u32[]{:S(2)}, u32[]{:S(2)}) collective-permute-start(f32[4,192,128]{2,1,0:T(8,128)S(1)} %get-tuple-element.456), channel_id=1, source_target_pairs={{4,0},{8,4},{12,8},{16,12},{20,16},{24,20},{28,24},{32,28},{36,32}... | collective-permute-start | bytes 1179656 | tf_op jit(solution)/shard_map/while/body/eval_jaxpr/ppermute | solution.py:18
  250.0 11.8 %copy-start.2 = (f32[8,192,128]{2,1,0:T(8,128)S(1)}, f32[8,192,128]{2,1,0:T(8,128)}, u32[]{:S(2)}) copy-start(f32[8,192,128]{2,1,0:T(8,128)} %get-tuple-element.485) | copy-start | bytes 2359300 | tf_op jit(solution)/shard_map/while
  275.3 10.3 %collective-permute-start.1 = (f32[4,192,128]{2,1,0:T(8,128)}, f32[4,192,128]{2,1,0:T(8,128)S(1)}, u32[]{:S(2)}, u32[]{:S(2)}) collective-permute-start(f32[4,192,128]{2,1,0:T(8,128)} %get-tuple-element.457), channel_id=1, source_target_pairs={{0,4},{4,8},{8,12},{12,16},{16,20},{20,24},{24,28},{28,32},{32,36}... | collective-permute-start | bytes 1179656 | tf_op jit(solution)/shard_map/while/body/eval_jaxpr/ppermute | solution.py:15
  280.6 16.2 %collective-permute-start = (f32[4,192,128]{2,1,0:T(8,128)S(1)}, f32[4,192,128]{2,1,0:T(8,128)S(1)}, u32[]{:S(2)}, u32[]{:S(2)}) collective-permute-start(f32[4,192,128]{2,1,0:T(8,128)S(1)} %get-tuple-element.456), channel_id=1, source_target_pairs={{4,0},{8,4},{12,8},{16,12},{20,16},{24,20},{28,24},{32,28},{36,32}... | collective-permute-start | bytes 1179656 | tf_op jit(solution)/shard_map/while/body/eval_jaxpr/ppermute | solution.py:18
  285.8 12.0 %copy-start.2 = (f32[8,192,128]{2,1,0:T(8,128)S(1)}, f32[8,192,128]{2,1,0:T(8,128)}, u32[]{:S(2)}) copy-start(f32[8,192,128]{2,1,0:T(8,128)} %get-tuple-element.485) | copy-start | bytes 2359300 | tf_op jit(solution)/shard_map/while
  311.3 10.3 %collective-permute-start.1 = (f32[4,192,128]{2,1,0:T(8,128)}, f32[4,192,128]{2,1,0:T(8,128)S(1)}, u32[]{:S(2)}, u32[]{:S(2)}) collective-permute-start(f32[4,192,128]{2,1,0:T(8,128)} %get-tuple-element.457), channel_id=1, source_target_pairs={{0,4},{4,8},{8,12},{12,16},{16,20},{20,24},{24,28},{28,32},{32,36}... | collective-permute-start | bytes 1179656 | tf_op jit(solution)/shard_map/while/body/eval_jaxpr/ppermute | solution.py:15
  316.6 15.3 %collective-permute-start = (f32[4,192,128]{2,1,0:T(8,128)S(1)}, f32[4,192,128]{2,1,0:T(8,128)S(1)}, u32[]{:S(2)}, u32[]{:S(2)}) collective-permute-start(f32[4,192,128]{2,1,0:T(8,128)S(1)} %get-tuple-element.456), channel_id=1, source_target_pairs={{4,0},{8,4},{12,8},{16,12},{20,16},{24,20},{28,24},{32,28},{36,32}... | collective-permute-start | bytes 1179656 | tf_op jit(solution)/shard_map/while/body/eval_jaxpr/ppermute | solution.py:18
  321.8 11.1 %copy-start.2 = (f32[8,192,128]{2,1,0:T(8,128)S(1)}, f32[8,192,128]{2,1,0:T(8,128)}, u32[]{:S(2)}) copy-start(f32[8,192,128]{2,1,0:T(8,128)} %get-tuple-element.485) | copy-start | bytes 2359300 | tf_op jit(solution)/shard_map/while
  347.0 9.8 %collective-permute-start.3 = (f32[4,192,128]{2,1,0:T(8,128)S(1)}, f32[4,192,128]{2,1,0:T(8,128)S(1)}, u32[]{:S(2)}, u32[]{:S(2)}) collective-permute-start(f32[4,192,128]{2,1,0:T(8,128)S(1)} %get-tuple-element.469), channel_id=1, source_target_pairs={{0,4},{4,8},{8,12},{12,16},{16,20},{20,24},{24,28},{28,32},{32,36}... | collective-permute-start | bytes 1179656 | tf_op jit(solution)/shard_map/while/body/eval_jaxpr/ppermute | solution.py:15
  352.0 11.4 %collective-permute-start.2 = (f32[4,192,128]{2,1,0:T(8,128)S(1)}, f32[4,192,128]{2,1,0:T(8,128)S(1)}, u32[]{:S(2)}, u32[]{:S(2)}) collective-permute-start(f32[4,192,128]{2,1,0:T(8,128)S(1)} %get-tuple-element.468), channel_id=1, source_target_pairs={{4,0},{8,4},{12,8},{16,12},{20,16},{24,20},{28,24},{32,28},{36,32}... | collective-permute-start | bytes 1179656 | tf_op jit(solution)/shard_map/while/body/eval_jaxpr/ppermute | solution.py:18
  375.1 20.0 %collective-permute-start.3 = (f32[4,192,128]{2,1,0:T(8,128)S(1)}, f32[4,192,128]{2,1,0:T(8,128)S(1)}, u32[]{:S(2)}, u32[]{:S(2)}) collective-permute-start(f32[4,192,128]{2,1,0:T(8,128)S(1)} %get-tuple-element.469), channel_id=1, source_target_pairs={{0,4},{4,8},{8,12},{12,16},{16,20},{20,24},{24,28},{28,32},{32,36}... | collective-permute-start | bytes 1179656 | tf_op jit(solution)/shard_map/while/body/eval_jaxpr/ppermute | solution.py:15
  380.4 20.0 %collective-permute-start.2 = (f32[4,192,128]{2,1,0:T(8,128)S(1)}, f32[4,192,128]{2,1,0:T(8,128)S(1)}, u32[]{:S(2)}, u32[]{:S(2)}) collective-permute-start(f32[4,192,128]{2,1,0:T(8,128)S(1)} %get-tuple-element.468), channel_id=1, source_target_pairs={{4,0},{8,4},{12,8},{16,12},{20,16},{24,20},{28,24},{32,28},{36,32}... | collective-permute-start | bytes 1179656 | tf_op jit(solution)/shard_map/while/body/eval_jaxpr/ppermute | solution.py:18
  412.1 10.6 %collective-permute-start.3 = (f32[4,192,128]{2,1,0:T(8,128)S(1)}, f32[4,192,128]{2,1,0:T(8,128)S(1)}, u32[]{:S(2)}, u32[]{:S(2)}) collective-permute-start(f32[4,192,128]{2,1,0:T(8,128)S(1)} %get-tuple-element.469), channel_id=1, source_target_pairs={{0,4},{4,8},{8,12},{12,16},{16,20},{20,24},{24,28},{28,32},{32,36}... | collective-permute-start | bytes 1179656 | tf_op jit(solution)/shard_map/while/body/eval_jaxpr/ppermute | solution.py:15
  417.3 16.0 %collective-permute-start.2 = (f32[4,192,128]{2,1,0:T(8,128)S(1)}, f32[4,192,128]{2,1,0:T(8,128)S(1)}, u32[]{:S(2)}, u32[]{:S(2)}) collective-permute-start(f32[4,192,128]{2,1,0:T(8,128)S(1)} %get-tuple-element.468), channel_id=1, source_target_pairs={{4,0},{8,4},{12,8},{16,12},{20,16},{24,20},{28,24},{32,28},{36,32}... | collective-permute-start | bytes 1179656 | tf_op jit(solution)/shard_map/while/body/eval_jaxpr/ppermute | solution.py:18
  422.9 11.5 %copy-start.3 = (f32[8,192,128]{2,1,0:T(8,128)S(1)}, f32[8,192,128]{2,1,0:T(8,128)}, u32[]{:S(2)}) copy-start(f32[8,192,128]{2,1,0:T(8,128)} %get-tuple-element.518) | copy-start | bytes 2359300 | tf_op jit(solution)/shard_map/while
  445.0 12.5 %collective-permute-start.3 = (f32[4,192,128]{2,1,0:T(8,128)S(1)}, f32[4,192,128]{2,1,0:T(8,128)S(1)}, u32[]{:S(2)}, u32[]{:S(2)}) collective-permute-start(f32[4,192,128]{2,1,0:T(8,128)S(1)} %get-tuple-element.469), channel_id=1, source_target_pairs={{0,4},{4,8},{8,12},{12,16},{16,20},{20,24},{24,28},{28,32},{32,36}... | collective-permute-start | bytes 1179656 | tf_op jit(solution)/shard_map/while/body/eval_jaxpr/ppermute | solution.py:15
  450.3 15.4 %collective-permute-start.2 = (f32[4,192,128]{2,1,0:T(8,128)S(1)}, f32[4,192,128]{2,1,0:T(8,128)S(1)}, u32[]{:S(2)}, u32[]{:S(2)}) collective-permute-start(f32[4,192,128]{2,1,0:T(8,128)S(1)} %get-tuple-element.468), channel_id=1, source_target_pairs={{4,0},{8,4},{12,8},{16,12},{20,16},{24,20},{28,24},{32,28},{36,32}... | collective-permute-start | bytes 1179656 | tf_op jit(solution)/shard_map/while/body/eval_jaxpr/ppermute | solution.py:18
  477.3 13.2 %collective-permute-start.3 = (f32[4,192,128]{2,1,0:T(8,128)S(1)}, f32[4,192,128]{2,1,0:T(8,128)S(1)}, u32[]{:S(2)}, u32[]{:S(2)}) collective-permute-start(f32[4,192,128]{2,1,0:T(8,128)S(1)} %get-tuple-element.469), channel_id=1, source_target_pairs={{0,4},{4,8},{8,12},{12,16},{16,20},{20,24},{24,28},{28,32},{32,36}... | collective-permute-start | bytes 1179656 | tf_op jit(solution)/shard_map/while/body/eval_jaxpr/ppermute | solution.py:15
  482.6 11.5 %collective-permute-start.2 = (f32[4,192,128]{2,1,0:T(8,128)S(1)}, f32[4,192,128]{2,1,0:T(8,128)S(1)}, u32[]{:S(2)}, u32[]{:S(2)}) collective-permute-start(f32[4,192,128]{2,1,0:T(8,128)S(1)} %get-tuple-element.468), channel_id=1, source_target_pairs={{4,0},{8,4},{12,8},{16,12},{20,16},{24,20},{28,24},{32,28},{36,32}... | collective-permute-start | bytes 1179656 | tf_op jit(solution)/shard_map/while/body/eval_jaxpr/ppermute | solution.py:18
  505.8 19.2 %collective-permute-start.3 = (f32[4,192,128]{2,1,0:T(8,128)S(1)}, f32[4,192,128]{2,1,0:T(8,128)S(1)}, u32[]{:S(2)}, u32[]{:S(2)}) collective-permute-start(f32[4,192,128]{2,1,0:T(8,128)S(1)} %get-tuple-element.469), channel_id=1, source_target_pairs={{0,4},{4,8},{8,12},{12,16},{16,20},{20,24},{24,28},{28,32},{32,36}... | collective-permute-start | bytes 1179656 | tf_op jit(solution)/shard_map/while/body/eval_jaxpr/ppermute | solution.py:15
  510.5 20.2 %collective-permute-start.2 = (f32[4,192,128]{2,1,0:T(8,128)S(1)}, f32[4,192,128]{2,1,0:T(8,128)S(1)}, u32[]{:S(2)}, u32[]{:S(2)}) collective-permute-start(f32[4,192,128]{2,1,0:T(8,128)S(1)} %get-tuple-element.468), channel_id=1, source_target_pairs={{4,0},{8,4},{12,8},{16,12},{20,16},{24,20},{28,24},{32,28},{36,32}... | collective-permute-start | bytes 1179656 | tf_op jit(solution)/shard_map/while/body/eval_jaxpr/ppermute | solution.py:18
  542.4 10.4 %collective-permute-start.3 = (f32[4,192,128]{2,1,0:T(8,128)S(1)}, f32[4,192,128]{2,1,0:T(8,128)S(1)}, u32[]{:S(2)}, u32[]{:S(2)}) collective-permute-start(f32[4,192,128]{2,1,0:T(8,128)S(1)} %get-tuple-element.469), channel_id=1, source_target_pairs={{0,4},{4,8},{8,12},{12,16},{16,20},{20,24},{24,28},{28,32},{32,36}... | collective-permute-start | bytes 1179656 | tf_op jit(solution)/shard_map/while/body/eval_jaxpr/ppermute | solution.py:15
  547.3 16.3 %collective-permute-start.2 = (f32[4,192,128]{2,1,0:T(8,128)S(1)}, f32[4,192,128]{2,1,0:T(8,128)S(1)}, u32[]{:S(2)}, u32[]{:S(2)}) collective-permute-start(f32[4,192,128]{2,1,0:T(8,128)S(1)} %get-tuple-element.468), channel_id=1, source_target_pairs={{4,0},{8,4},{12,8},{16,12},{20,16},{24,20},{28,24},{32,28},{36,32}... | collective-permute-start | bytes 1179656 | tf_op jit(solution)/shard_map/while/body/eval_jaxpr/ppermute | solution.py:18
  553.0 11.7 %copy-start.3 = (f32[8,192,128]{2,1,0:T(8,128)S(1)}, f32[8,192,128]{2,1,0:T(8,128)}, u32[]{:S(2)}) copy-start(f32[8,192,128]{2,1,0:T(8,128)} %get-tuple-element.518) | copy-start | bytes 2359300 | tf_op jit(solution)/shard_map/while
  575.4 12.3 %collective-permute-start.3 = (f32[4,192,128]{2,1,0:T(8,128)S(1)}, f32[4,192,128]{2,1,0:T(8,128)S(1)}, u32[]{:S(2)}, u32[]{:S(2)}) collective-permute-start(f32[4,192,128]{2,1,0:T(8,128)S(1)} %get-tuple-element.469), channel_id=1, source_target_pairs={{0,4},{4,8},{8,12},{12,16},{16,20},{20,24},{24,28},{28,32},{32,36}... | collective-permute-start | bytes 1179656 | tf_op jit(solution)/shard_map/while/body/eval_jaxpr/ppermute | solution.py:15
  580.3 15.4 %collective-permute-start.2 = (f32[4,192,128]{2,1,0:T(8,128)S(1)}, f32[4,192,128]{2,1,0:T(8,128)S(1)}, u32[]{:S(2)}, u32[]{:S(2)}) collective-permute-start(f32[4,192,128]{2,1,0:T(8,128)S(1)} %get-tuple-element.468), channel_id=1, source_target_pairs={{4,0},{8,4},{12,8},{16,12},{20,16},{24,20},{28,24},{32,28},{36,32}... | collective-permute-start | bytes 1179656 | tf_op jit(solution)/shard_map/while/body/eval_jaxpr/ppermute | solution.py:18
  607.4 13.2 %collective-permute-start.3 = (f32[4,192,128]{2,1,0:T(8,128)S(1)}, f32[4,192,128]{2,1,0:T(8,128)S(1)}, u32[]{:S(2)}, u32[]{:S(2)}) collective-permute-start(f32[4,192,128]{2,1,0:T(8,128)S(1)} %get-tuple-element.469), channel_id=1, source_target_pairs={{0,4},{4,8},{8,12},{12,16},{16,20},{20,24},{24,28},{28,32},{32,36}... | collective-permute-start | bytes 1179656 | tf_op jit(solution)/shard_map/while/body/eval_jaxpr/ppermute | solution.py:15
  612.7 11.5 %collective-permute-start.2 = (f32[4,192,128]{2,1,0:T(8,128)S(1)}, f32[4,192,128]{2,1,0:T(8,128)S(1)}, u32[]{:S(2)}, u32[]{:S(2)}) collective-permute-start(f32[4,192,128]{2,1,0:T(8,128)S(1)} %get-tuple-element.468), channel_id=1, source_target_pairs={{4,0},{8,4},{12,8},{16,12},{20,16},{24,20},{28,24},{32,28},{36,32}... | collective-permute-start | bytes 1179656 | tf_op jit(solution)/shard_map/while/body/eval_jaxpr/ppermute | solution.py:18
  635.9 19.2 %collective-permute-start.3 = (f32[4,192,128]{2,1,0:T(8,128)S(1)}, f32[4,192,128]{2,1,0:T(8,128)S(1)}, u32[]{:S(2)}, u32[]{:S(2)}) collective-permute-start(f32[4,192,128]{2,1,0:T(8,128)S(1)} %get-tuple-element.469), channel_id=1, source_target_pairs={{0,4},{4,8},{8,12},{12,16},{16,20},{20,24},{24,28},{28,32},{32,36}... | collective-permute-start | bytes 1179656 | tf_op jit(solution)/shard_map/while/body/eval_jaxpr/ppermute | solution.py:15
  640.6 20.2 %collective-permute-start.2 = (f32[4,192,128]{2,1,0:T(8,128)S(1)}, f32[4,192,128]{2,1,0:T(8,128)S(1)}, u32[]{:S(2)}, u32[]{:S(2)}) collective-permute-start(f32[4,192,128]{2,1,0:T(8,128)S(1)} %get-tuple-element.468), channel_id=1, source_target_pairs={{4,0},{8,4},{12,8},{16,12},{20,16},{24,20},{28,24},{32,28},{36,32}... | collective-permute-start | bytes 1179656 | tf_op jit(solution)/shard_map/while/body/eval_jaxpr/ppermute | solution.py:18
  (50 other events, 216.8 us)
Sparse Core Ops, SparseCore 0:
  672.6 91.8 all-reduce.3
where the time goes:
time: 777 us; the launch traced here: 773 us
  waiting for transfers between devices  349 us (45%)
  other arithmetic  200 us (26%)
  starting transfers between devices  110 us (14%)
  local copies, waits for them, and re-layouts  97.8 us (13%)
  between operations  14.1 us (2%)
    ppermute x20, waiting for transfers between devices, with_halo(): lax.ppermute(lax.slice_in_dim(block, 0, width, axis=dim), axis, backward)  164 us
    ppermute x20, waiting for transfers between devices, with_halo(): lax.ppermute(lax.slice_in_dim(block, block.shape[dim] - width, None, axis...  93.5 us
    psum x1, waiting for transfers between devices, per_device(): summed = lax.psum(imaging, 'shot')  92 us
    ppermute x20, starting transfers between devices, with_halo(): lax.ppermute(lax.slice_in_dim(block, block.shape[dim] - width, None, axis...  84.1 us
    scatter-add x10, other arithmetic, backward(): earlier.reshape(-1).at[receiver_cells].add(residual).reshape(velocity.shape)  37.4 us
    add x10, other arithmetic, forward(): latest = 2.0 * current - former + courant_sq * laplace(edge_layers(current))  32.8 us
    add x10, other arithmetic, backward(): 2.0 * following - furthest + courant_sq * laplace(edge_layers(following))  32.8 us
    while x180, local copies, waits for them, and re-layouts  32.6 us
  transfers between devices with their start and end apart: 41, of which 41 were waited for; matrix products, arithmetic and copies ran while one was open for 4% of the time, Pallas kernels for 0%

commit v1 on v0

v1 whole, which is shorter than its diff:
```python
import jax
import jax.numpy as jnp
from jax import lax
from jax.sharding import PartitionSpec as P

TAPS = (-205.0 / 72.0, 8.0 / 5.0, -1.0 / 5.0, 8.0 / 315.0, -1.0 / 560.0)
COURANT = 0.09
RADIUS = 4


def exchange_edges(block):
    count = lax.axis_size("space")
    forward = [(i, i + 1) for i in range(count - 1)]
    backward = [(target, source) for source, target in forward]
    low = lax.ppermute(block[block.shape[0] - RADIUS :], "space", forward)
    high = lax.ppermute(block[:RADIUS], "space", backward)
    return low, high


def inner_laplace(block):
    length_x, extent_y, extent_z = block.shape
    padded = jnp.pad(block, ((4, 4), (4, 4), (4, 4)))
    result = 3.0 * TAPS[0] * block
    for distance in range(1, 5):
        beside_all = (
            padded[4 + distance : 4 + distance + length_x, 4 : 4 + extent_y, 4 : 4 + extent_z]
            + padded[4 - distance : 4 - distance + length_x, 4 : 4 + extent_y, 4 : 4 + extent_z]
        )
        beside_all = (
            beside_all
            + padded[4 : 4 + length_x, 4 + distance : 4 + distance + extent_y, 4 : 4 + extent_z]
            + padded[4 : 4 + length_x, 4 - distance : 4 - distance + extent_y, 4 : 4 + extent_z]
        )
        beside_all = (
            beside_all
            + padded[4 : 4 + length_x, 4 : 4 + extent_y, 4 + distance : 4 + distance + extent_z]
            + padded[4 : 4 + length_x, 4 : 4 + extent_y, 4 - distance : 4 - distance + extent_z]
        )
        result = result + TAPS[distance] * beside_all
    return result


def edge_terms(low, high, length_x):
    middle = jnp.zeros((length_x,) + low.shape[1:], low.dtype)
    widened = jnp.concatenate([low, middle, high], axis=0)
    result = None
    for distance in range(1, 5):
        beside = (
            widened[4 + distance : 4 + distance + length_x]
            + widened[4 - distance : 4 - distance + length_x]
        )
        term = TAPS[distance] * beside
        result = term if result is None else result + term
    return result


def step(current, former, courant_sq, injected):
    low, high = exchange_edges(current)
    interior = inner_laplace(current)
    lap = interior + edge_terms(low, high, current.shape[0])
    return 2.0 * current - former + courant_sq * lap + injected


def per_device(
    velocity,
    wave_now,
    wave_prev,
    adjoint_now,
    adjoint_prev,
    source_cells,
    wavelet,
    receiver_cells,
    receiver_counts,
    observed,
):
    extent_x, extent_y, extent_z = velocity.shape
    block_cells = extent_x * extent_y * extent_z
    steps = wavelet.shape[1]
    courant_sq = (COURANT * velocity) ** 2
    position = lax.axis_index("space")
    local_sources = source_cells[0] - position * block_cells
    inside = (local_sources >= 0) & (local_sources < block_cells)
    source_index = jnp.where(inside, local_sources, 0)
    pulses = wavelet[0]
    empty_flat = jnp.zeros((block_cells,), jnp.float32)

    current, former = wave_now[0], wave_prev[0]
    accelerations = []
    traces = []
    for t in range(steps):
        injected = empty_flat.at[source_index].add(jnp.where(inside, pulses[t], 0.0))
        latest = step(current, former, courant_sq, injected.reshape(velocity.shape))
        accelerations.append(latest - 2.0 * current + former)
        traces.append(latest.reshape(-1)[receiver_cells])
        current, former = latest, current

    live_slots = (jnp.arange(receiver_cells.shape[0], dtype=jnp.int32) < receiver_counts[0]).astype(
        jnp.float32
    )
    misfit = [(traces[t] - observed[0, t]) * live_slots for t in range(steps)]

    following, furthest = adjoint_now[0], adjoint_prev[0]
    imaging = jnp.zeros_like(velocity)
    for t in reversed(range(steps)):
        injected = empty_flat.at[receiver_cells].add(misfit[t])
        earlier = step(following, furthest, courant_sq, injected.reshape(velocity.shape))
        imaging = imaging + earlier * accelerations[t]
        following, furthest = earlier, following

    shots = lax.axis_size("shot")
    shot = lax.axis_index("shot")
    band_rows = extent_y // shots
    core = shot % 2
    half = shot // 2
    banded = imaging.reshape(extent_x, 2, 2, band_rows, extent_z)
    kept = lax.dynamic_index_in_dim(banded, core, axis=2, keepdims=False)
    sent = lax.dynamic_index_in_dim(banded, 1 - core, axis=2, keepdims=False)
    summed = kept + lax.ppermute(sent, "shot", [(s, s ^ 1) for s in range(shots)])
    kept = lax.dynamic_index_in_dim(summed, half, axis=1, keepdims=False)
    sent = lax.dynamic_index_in_dim(summed, 1 - half, axis=1, keepdims=False)
    own_band = kept + lax.ppermute(sent, "shot", [(s, s ^ 2) for s in range(shots)])

    offset = shot * band_rows
    factor = lax.dynamic_slice_in_dim(-2.0 / velocity**3, offset, band_rows, 1)
    return factor * own_band


def solution(mesh):
    in_specs = (
        P("space", None, None),
        P("shot", "space", None, None),
        P("shot", "space", None, None),
        P("shot", "space", None, None),
        P("shot", "space", None, None),
        P("shot", None),
        P("shot", None, None),
        P("space"),
        P("space"),
        P("shot", None, "space"),
    )
    out_specs = P("space", "shot", None)
    return jax.shard_map(
        per_device, mesh=mesh, in_specs=in_specs, out_specs=out_specs, check_vma=False
    )
```

time: 777 us -> 586 us (0.75)
  the two profiles are of different devices: /device:TPU:1 before, /device:TPU:46 now
where the time goes in v1:
time: 586 us; the launch traced here: 576 us
  waiting for transfers between devices  186 us (32%)
  other arithmetic  173 us (30%)
  starting transfers between devices  141 us (24%)
  local copies, waits for them, and re-layouts  73.9 us (13%)
    ppermute x20, waiting for transfers between devices, exchange_edges(): low = lax.ppermute(block[block.shape[0] - RADIUS:], 'space', forward)  104 us
    ppermute x20, starting transfers between devices, exchange_edges(): low = lax.ppermute(block[block.shape[0] - RADIUS:], 'space', forward)  90.4 us
    add x19, other arithmetic, step(): return 2.0 * current - former + courant_sq * lap + injected  85 us
    ppermute x20, waiting for transfers between devices, exchange_edges(): high = lax.ppermute(block[:RADIUS], 'space', backward)  73.4 us
    ppermute x20, starting transfers between devices, exchange_edges(): high = lax.ppermute(block[:RADIUS], 'space', backward)  45.1 us
    gather x10, local copies, waits for them, and re-layouts, per_device(): traces.append(latest.reshape(-1)[receiver_cells])  43.8 us
    scatter-add x10, other arithmetic, per_device(): injected = empty_flat.at[receiver_cells].add(misfit[t])  43 us
    scatter-add x10, other arithmetic, per_device(): empty_flat.at[source_index].add(jnp.where(inside, pulses[t], 0.0))  20.9 us
  transfers between devices with their start and end apart: 42, of which 34 were waited for; matrix products, arithmetic and copies ran while one was open for 22% of the time, Pallas kernels for 0%

profile of v1, /device:TPU:46, one launch (start us, length us, event | category | flops | bytes accessed | tf_op | source)
XLA Modules:
  0.0 575.7 jit_solution(14861312306326134391)
XLA Ops:
  12.7 4.5 collective-permute-done.2
  17.2 6.3 %collective-permute-done.3 = f32[4,192,128]{2,1,0:T(8,128)S(1)} collective-permute-done((f32[4,192,128]{2,1,0:T(8,128)S(1)}, f32[4,192,128]{2,1,0:T(8,128)S(1)}, u32[]{:S(2)}, u32[]{:S(2)}) %collective-permute-start.3) | collective-permute-done | bytes 393248 | tf_op jit(solution)/shard_map/ppermute | solution.py:15
  37.7 5.8 %collective-permute-done.4 = f32[4,192,128]{2,1,0:T(8,128)S(1)} collective-permute-done((f32[4,192,128]{2,1,0:T(8,128)}, f32[4,192,128]{2,1,0:T(8,128)S(1)}, u32[]{:S(2)}, u32[]{:S(2)}) %collective-permute-start.4) | collective-permute-done | bytes 393248 | tf_op jit(solution)/shard_map/ppermute | solution.py:16
  43.6 9.9 %collective-permute-done.5 = f32[4,192,128]{2,1,0:T(8,128)S(1)} collective-permute-done((f32[4,192,128]{2,1,0:T(8,128)S(1)}, f32[4,192,128]{2,1,0:T(8,128)S(1)}, u32[]{:S(2)}, u32[]{:S(2)}) %collective-permute-start.5) | collective-permute-done | bytes 393248 | tf_op jit(solution)/shard_map/ppermute | solution.py:15
  60.6 4.5 collective-permute-start.7
  67.0 6.5 %collective-permute-done.6 = f32[4,192,128]{2,1,0:T(8,128)S(1)} collective-permute-done((f32[4,192,128]{2,1,0:T(8,128)}, f32[4,192,128]{2,1,0:T(8,128)S(1)}, u32[]{:S(2)}, u32[]{:S(2)}) %collective-permute-start.6) | collective-permute-done | bytes 393248 | tf_op jit(solution)/shard_map/ppermute | solution.py:16
  73.5 5.7 collective-permute-done.7
  86.4 4.5 collective-permute-start.9
  92.8 6.5 %collective-permute-done.8 = f32[4,192,128]{2,1,0:T(8,128)S(1)} collective-permute-done((f32[4,192,128]{2,1,0:T(8,128)}, f32[4,192,128]{2,1,0:T(8,128)S(1)}, u32[]{:S(2)}, u32[]{:S(2)}) %collective-permute-start.8) | collective-permute-done | bytes 393248 | tf_op jit(solution)/shard_map/ppermute | solution.py:16
  99.3 5.6 collective-permute-done.9
  112.2 4.5 collective-permute-start.11
  118.6 6.5 %collective-permute-done.10 = f32[4,192,128]{2,1,0:T(8,128)S(1)} collective-permute-done((f32[4,192,128]{2,1,0:T(8,128)}, f32[4,192,128]{2,1,0:T(8,128)S(1)}, u32[]{:S(2)}, u32[]{:S(2)}) %collective-permute-start.10) | collective-permute-done | bytes 393248 | tf_op jit(solution)/shard_map/ppermute | solution.py:16
  125.1 6.9 %collective-permute-done.11 = f32[4,192,128]{2,1,0:T(8,128)S(1)} collective-permute-done((f32[4,192,128]{2,1,0:T(8,128)S(1)}, f32[4,192,128]{2,1,0:T(8,128)S(1)}, u32[]{:S(2)}, u32[]{:S(2)}) %collective-permute-start.11) | collective-permute-done | bytes 393248 | tf_op jit(solution)/shard_map/ppermute | solution.py:15
  139.3 4.5 collective-permute-start.13
  145.8 6.3 %collective-permute-done.12 = f32[4,192,128]{2,1,0:T(8,128)S(1)} collective-permute-done((f32[4,192,128]{2,1,0:T(8,128)}, f32[4,192,128]{2,1,0:T(8,128)S(1)}, u32[]{:S(2)}, u32[]{:S(2)}) %collective-permute-start.12) | collective-permute-done | bytes 393248 | tf_op jit(solution)/shard_map/ppermute | solution.py:16
  152.2 5.8 %collective-permute-done.13 = f32[4,192,128]{2,1,0:T(8,128)S(1)} collective-permute-done((f32[4,192,128]{2,1,0:T(8,128)S(1)}, f32[4,192,128]{2,1,0:T(8,128)S(1)}, u32[]{:S(2)}, u32[]{:S(2)}) %collective-permute-start.13) | collective-permute-done | bytes 393248 | tf_op jit(solution)/shard_map/ppermute | solution.py:15
  165.3 4.5 collective-permute-start.15
  171.6 6.5 %collective-permute-done.14 = f32[4,192,128]{2,1,0:T(8,128)S(1)} collective-permute-done((f32[4,192,128]{2,1,0:T(8,128)}, f32[4,192,128]{2,1,0:T(8,128)S(1)}, u32[]{:S(2)}, u32[]{:S(2)}) %collective-permute-start.14) | collective-permute-done | bytes 393248 | tf_op jit(solution)/shard_map/ppermute | solution.py:16
  178.1 5.7 collective-permute-done.15
  191.1 4.5 collective-permute-start.17
  197.5 6.5 %collective-permute-done.16 = f32[4,192,128]{2,1,0:T(8,128)S(1)} collective-permute-done((f32[4,192,128]{2,1,0:T(8,128)}, f32[4,192,128]{2,1,0:T(8,128)S(1)}, u32[]{:S(2)}, u32[]{:S(2)}) %collective-permute-start.16) | collective-permute-done | bytes 393248 | tf_op jit(solution)/shard_map/ppermute | solution.py:16
  204.0 5.6 collective-permute-done.17
  217.1 4.5 collective-permute-start.19
  231.8 7.1 %collective-permute-done.19 = f32[4,192,128]{2,1,0:T(8,128)S(1)} collective-permute-done((f32[4,192,128]{2,1,0:T(8,128)}, f32[4,192,128]{2,1,0:T(8,128)S(1)}, u32[]{:S(2)}, u32[]{:S(2)}) %collective-permute-start.19) | collective-permute-done | bytes 393248 | tf_op jit(solution)/shard_map/ppermute | solution.py:15
  246.3 4.8 collective-permute-start.21
  263.7 9.0 %collective-permute-done.21 = f32[4,192,128]{2,1,0:T(8,128)} collective-permute-done((f32[4,192,128]{2,1,0:T(8,128)}, f32[4,192,128]{2,1,0:T(8,128)}, u32[]{:S(2)}, u32[]{:S(2)}) %collective-permute-start.21) | collective-permute-done | bytes 393248 | tf_op jit(solution)/shard_map/ppermute | solution.py:15
  277.1 6.5 %gather_fusion = f32[512]{0:T(512)S(1)} fusion(f32[196608]{0:T(1024)} %bitcast.126, s32[1024]{0:T(1024)S(1)} %pad_clamp_fusion), kind=kCustom, calls=%fused_computation | custom fusion | bytes 6144 | tf_op jit(solution)/shard_map/gather | solution.py:94
  284.2 4.6 scatter_custom_fusion.10
  288.8 12.6 %fusion.8 = f32[8,192,128]{2,1,0:T(8,128)S(1)} fusion(f32[8,192,128]{2,1,0:T(8,128)} %bitcast.141, f32[4,192,128]{2,1,0:T(8,128)S(1)} %collective-permute-done, f32[4,192,128]{2,1,0:T(8,128)} %collective-permute-done.1, f32[8,192,128]{2,1,0:T(8,128)} %bitcast.128, f32[1,8,192,128]{3,2,1,0:T(8,128)} %param.14, f32[8,192,128]{2,1,0:T(8,128)S(1)} %copy-done), kind=kLoop, calls=%fused_computation.678 | loop fusion | flops 9437184 | bytes 4718592 | tf_op jit(solution)/shard_map/add | solution.py:61
  304.6 4.6 collective-permute-start.23
  317.6 5.8 %collective-permute-done.23 = f32[4,192,128]{2,1,0:T(8,128)} collective-permute-done((f32[4,192,128]{2,1,0:T(8,128)}, f32[4,192,128]{2,1,0:T(8,128)}, u32[]{:S(2)}, u32[]{:S(2)}) %collective-permute-start.23) | collective-permute-done | bytes 393248 | tf_op jit(solution)/shard_map/ppermute | solution.py:15
  330.2 4.5 collective-permute-start.25
  355.3 4.6 collective-permute-start.27
  368.2 5.7 collective-permute-done.27
  381.2 4.9 collective-permute-start.29
  408.1 4.5 collective-permute-start.31
  416.3 4.7 collective-permute-done.30
  421.0 7.0 %collective-permute-done.31 = f32[4,192,128]{2,1,0:T(8,128)} collective-permute-done((f32[4,192,128]{2,1,0:T(8,128)}, f32[4,192,128]{2,1,0:T(8,128)}, u32[]{:S(2)}, u32[]{:S(2)}) %collective-permute-start.31) | collective-permute-done | bytes 393248 | tf_op jit(solution)/shard_map/ppermute | solution.py:15
  434.8 4.5 collective-permute-start.33
  462.6 4.5 collective-permute-start.35
  475.4 6.6 %collective-permute-done.35 = f32[4,192,128]{2,1,0:T(8,128)} collective-permute-done((f32[4,192,128]{2,1,0:T(8,128)}, f32[4,192,128]{2,1,0:T(8,128)}, u32[]{:S(2)}, u32[]{:S(2)}) %collective-permute-start.35) | collective-permute-done | bytes 393248 | tf_op jit(solution)/shard_map/ppermute | solution.py:15
  488.8 4.7 collective-permute-start.37
  502.2 4.4 scatter_custom_fusion.18
  509.1 13.4 %fusion.278 = f32[8,192,128]{2,1,0:T(8,128)S(1)} fusion(f32[8,192,128]{2,1,0:T(8,128)} %bitcast.149, f32[4,192,128]{2,1,0:T(8,128)S(1)} %collective-permute-done.36, f32[4,192,128]{2,1,0:T(8,128)} %collective-permute-done.37, f32[8,192,128]{2,1,0:T(8,128)} %copy-done.29, f32[8,192,128]{2,1,0:T(8,128)} %copy-done.26, f32[8,192,128]{2,1,0:T(8,128)S(1)} %copy-done), kind=kLoop, calls=%fused_computation.948 | loop fusion | flops 9437184 | bytes 4718592 | tf_op jit(solution)/shard_map/add | solution.py:61
  525.7 4.5 collective-permute-start.39
  538.6 5.8 %collective-permute-done.39 = f32[4,192,128]{2,1,0:T(8,128)} collective-permute-done((f32[4,192,128]{2,1,0:T(8,128)S(1)}, f32[4,192,128]{2,1,0:T(8,128)}, u32[]{:S(2)}, u32[]{:S(2)}) %collective-permute-start.39) | collective-permute-done | bytes 393248 | tf_op jit(solution)/shard_map/ppermute | solution.py:15
  544.4 16.2 %fusion.295 = f32[8,192,128]{2,1,0:T(8,128)S(1)} fusion(f32[8,192,128]{2,1,0:T(8,128)} %bitcast.129, f32[4,192,128]{2,1,0:T(8,128)} %collective-permute-done.38, f32[4,192,128]{2,1,0:T(8,128)} %collective-permute-done.39, f32[8,192,128]{2,1,0:T(8,128)} %copy-done.30, f32[1,8,192,128]{3,2,1,0:T(8,128)} %param.12, f32[8,192,128]{2,1,0:T(8,128)S(1)} %copy-done.2, ...), kind=kLoop, calls=%fused_computation.965 | loop fusion | flops 19070976 | bytes 19660800 | tf_op jit(solution)/shard_map/add | solution.py:107
  567.8 7.0 %collective-permute-done.41 = f32[8,48,128]{2,1,0:T(8,128)S(1)} collective-permute-done((f32[8,48,128]{2,1,0:T(8,128)S(1)}, f32[8,48,128]{2,1,0:T(8,128)S(1)}, u32[]{:S(2)}, u32[]{:S(2)}) %collective-permute-start.41) | collective-permute-done | bytes 196640 | tf_op jit(solution)/shard_map/ppermute | solution.py:121
  (224 shorter events, 278.3 us)
Async XLA Ops:
  2.1 15.1 %collective-permute-start.2 = (f32[4,192,128]{2,1,0:T(8,128)}, f32[4,192,128]{2,1,0:T(8,128)S(1)}, u32[]{:S(2)}, u32[]{:S(2)}) collective-permute-start(f32[4,192,128]{2,1,0:T(8,128)} %get-tuple-element.48), channel_id=1, source_target_pairs={{4,0},{8,4},{12,8},{16,12},{20,16},{24,20},{28,24},{32,28},{36,32}... | collective-permute-start | bytes 1179656 | tf_op jit(solution)/shard_map/ppermute | solution.py:16
  4.9 18.5 %collective-permute-start.3 = (f32[4,192,128]{2,1,0:T(8,128)S(1)}, f32[4,192,128]{2,1,0:T(8,128)S(1)}, u32[]{:S(2)}, u32[]{:S(2)}) collective-permute-start(f32[4,192,128]{2,1,0:T(8,128)S(1)} %get-tuple-element.47), channel_id=1, source_target_pairs={{0,4},{4,8},{8,12},{12,16},{16,20},{20,24},{24,28},{28,32},{32,36}... | collective-permute-start | bytes 1179656 | tf_op jit(solution)/shard_map/ppermute | solution.py:15
  27.6 26.6 %copy-start.1 = (f32[8,192,128]{2,1,0:T(8,128)}, f32[8,192,128]{2,1,0:T(8,128)S(1)}, u32[]{:S(2)}) copy-start(f32[8,192,128]{2,1,0:T(8,128)S(1)} %fusion.23) | copy-start | bytes 2359300
  28.5 15.0 %collective-permute-start.4 = (f32[4,192,128]{2,1,0:T(8,128)}, f32[4,192,128]{2,1,0:T(8,128)S(1)}, u32[]{:S(2)}, u32[]{:S(2)}) collective-permute-start(f32[4,192,128]{2,1,0:T(8,128)} %get-tuple-element.46), channel_id=1, source_target_pairs={{4,0},{8,4},{12,8},{16,12},{20,16},{24,20},{28,24},{32,28},{36,32}... | collective-permute-start | bytes 1179656 | tf_op jit(solution)/shard_map/ppermute | solution.py:16
  31.2 22.2 %collective-permute-start.5 = (f32[4,192,128]{2,1,0:T(8,128)S(1)}, f32[4,192,128]{2,1,0:T(8,128)S(1)}, u32[]{:S(2)}, u32[]{:S(2)}) collective-permute-start(f32[4,192,128]{2,1,0:T(8,128)S(1)} %get-tuple-element.45), channel_id=1, source_target_pairs={{0,4},{4,8},{8,12},{12,16},{16,20},{20,24},{24,28},{28,32},{32,36}... | collective-permute-start | bytes 1179656 | tf_op jit(solution)/shard_map/ppermute | solution.py:15
  58.4 15.0 %collective-permute-start.6 = (f32[4,192,128]{2,1,0:T(8,128)}, f32[4,192,128]{2,1,0:T(8,128)S(1)}, u32[]{:S(2)}, u32[]{:S(2)}) collective-permute-start(f32[4,192,128]{2,1,0:T(8,128)} %get-tuple-element.44), channel_id=1, source_target_pairs={{4,0},{8,4},{12,8},{16,12},{20,16},{24,20},{28,24},{32,28},{36,32}... | collective-permute-start | bytes 1179656 | tf_op jit(solution)/shard_map/ppermute | solution.py:16
  60.6 18.5 %collective-permute-start.7 = (f32[4,192,128]{2,1,0:T(8,128)S(1)}, f32[4,192,128]{2,1,0:T(8,128)S(1)}, u32[]{:S(2)}, u32[]{:S(2)}) collective-permute-start(f32[4,192,128]{2,1,0:T(8,128)S(1)} %get-tuple-element.43), channel_id=1, source_target_pairs={{0,4},{4,8},{8,12},{12,16},{16,20},{20,24},{24,28},{28,32},{32,36}... | collective-permute-start | bytes 1179656 | tf_op jit(solution)/shard_map/ppermute | solution.py:15
  84.2 15.0 %collective-permute-start.8 = (f32[4,192,128]{2,1,0:T(8,128)}, f32[4,192,128]{2,1,0:T(8,128)S(1)}, u32[]{:S(2)}, u32[]{:S(2)}) collective-permute-start(f32[4,192,128]{2,1,0:T(8,128)} %get-tuple-element.42), channel_id=1, source_target_pairs={{4,0},{8,4},{12,8},{16,12},{20,16},{24,20},{28,24},{32,28},{36,32}... | collective-permute-start | bytes 1179656 | tf_op jit(solution)/shard_map/ppermute | solution.py:16
  86.4 18.5 %collective-permute-start.9 = (f32[4,192,128]{2,1,0:T(8,128)S(1)}, f32[4,192,128]{2,1,0:T(8,128)S(1)}, u32[]{:S(2)}, u32[]{:S(2)}) collective-permute-start(f32[4,192,128]{2,1,0:T(8,128)S(1)} %get-tuple-element.41), channel_id=1, source_target_pairs={{0,4},{4,8},{8,12},{12,16},{16,20},{20,24},{24,28},{28,32},{32,36}... | collective-permute-start | bytes 1179656 | tf_op jit(solution)/shard_map/ppermute | solution.py:15
  110.0 15.0 %collective-permute-start.10 = (f32[4,192,128]{2,1,0:T(8,128)}, f32[4,192,128]{2,1,0:T(8,128)S(1)}, u32[]{:S(2)}, u32[]{:S(2)}) collective-permute-start(f32[4,192,128]{2,1,0:T(8,128)} %get-tuple-element.40), channel_id=1, source_target_pairs={{4,0},{8,4},{12,8},{16,12},{20,16},{24,20},{28,24},{32,28},{36,32}... | collective-permute-start | bytes 1179656 | tf_op jit(solution)/shard_map/ppermute | solution.py:16
  112.2 19.8 %collective-permute-start.11 = (f32[4,192,128]{2,1,0:T(8,128)S(1)}, f32[4,192,128]{2,1,0:T(8,128)S(1)}, u32[]{:S(2)}, u32[]{:S(2)}) collective-permute-start(f32[4,192,128]{2,1,0:T(8,128)S(1)} %get-tuple-element.39), channel_id=1, source_target_pairs={{0,4},{4,8},{8,12},{12,16},{16,20},{20,24},{24,28},{28,32},{32,36}... | collective-permute-start | bytes 1179656 | tf_op jit(solution)/shard_map/ppermute | solution.py:15
  137.1 15.0 %collective-permute-start.12 = (f32[4,192,128]{2,1,0:T(8,128)}, f32[4,192,128]{2,1,0:T(8,128)S(1)}, u32[]{:S(2)}, u32[]{:S(2)}) collective-permute-start(f32[4,192,128]{2,1,0:T(8,128)} %get-tuple-element.38), channel_id=1, source_target_pairs={{4,0},{8,4},{12,8},{16,12},{20,16},{24,20},{28,24},{32,28},{36,32}... | collective-permute-start | bytes 1179656 | tf_op jit(solution)/shard_map/ppermute | solution.py:16
  139.3 18.6 %collective-permute-start.13 = (f32[4,192,128]{2,1,0:T(8,128)S(1)}, f32[4,192,128]{2,1,0:T(8,128)S(1)}, u32[]{:S(2)}, u32[]{:S(2)}) collective-permute-start(f32[4,192,128]{2,1,0:T(8,128)S(1)} %get-tuple-element.37), channel_id=1, source_target_pairs={{0,4},{4,8},{8,12},{12,16},{16,20},{20,24},{24,28},{28,32},{32,36}... | collective-permute-start | bytes 1179656 | tf_op jit(solution)/shard_map/ppermute | solution.py:15
  163.1 15.0 %collective-permute-start.14 = (f32[4,192,128]{2,1,0:T(8,128)}, f32[4,192,128]{2,1,0:T(8,128)S(1)}, u32[]{:S(2)}, u32[]{:S(2)}) collective-permute-start(f32[4,192,128]{2,1,0:T(8,128)} %get-tuple-element.36), channel_id=1, source_target_pairs={{4,0},{8,4},{12,8},{16,12},{20,16},{24,20},{28,24},{32,28},{36,32}... | collective-permute-start | bytes 1179656 | tf_op jit(solution)/shard_map/ppermute | solution.py:16
  165.3 18.5 %collective-permute-start.15 = (f32[4,192,128]{2,1,0:T(8,128)S(1)}, f32[4,192,128]{2,1,0:T(8,128)S(1)}, u32[]{:S(2)}, u32[]{:S(2)}) collective-permute-start(f32[4,192,128]{2,1,0:T(8,128)S(1)} %get-tuple-element.35), channel_id=1, source_target_pairs={{0,4},{4,8},{8,12},{12,16},{16,20},{20,24},{24,28},{28,32},{32,36}... | collective-permute-start | bytes 1179656 | tf_op jit(solution)/shard_map/ppermute | solution.py:15
  188.1 146.7 %copy-start.13 = (f32[8,192,128]{2,1,0:T(8,128)}, f32[8,192,128]{2,1,0:T(8,128)S(1)}, u32[]{:S(2)}) copy-start(f32[8,192,128]{2,1,0:T(8,128)S(1)} %fusion.113) | copy-start | bytes 2359300
  188.9 15.0 %collective-permute-start.16 = (f32[4,192,128]{2,1,0:T(8,128)}, f32[4,192,128]{2,1,0:T(8,128)S(1)}, u32[]{:S(2)}, u32[]{:S(2)}) collective-permute-start(f32[4,192,128]{2,1,0:T(8,128)} %get-tuple-element.34), channel_id=1, source_target_pairs={{4,0},{8,4},{12,8},{16,12},{20,16},{24,20},{28,24},{32,28},{36,32}... | collective-permute-start | bytes 1179656 | tf_op jit(solution)/shard_map/ppermute | solution.py:16
  191.1 18.5 %collective-permute-start.17 = (f32[4,192,128]{2,1,0:T(8,128)S(1)}, f32[4,192,128]{2,1,0:T(8,128)S(1)}, u32[]{:S(2)}, u32[]{:S(2)}) collective-permute-start(f32[4,192,128]{2,1,0:T(8,128)S(1)} %get-tuple-element.33), channel_id=1, source_target_pairs={{0,4},{4,8},{8,12},{12,16},{16,20},{20,24},{24,28},{28,32},{32,36}... | collective-permute-start | bytes 1179656 | tf_op jit(solution)/shard_map/ppermute | solution.py:15
  213.8 125.1 %copy-start.14 = (f32[8,192,128]{2,1,0:T(8,128)}, f32[8,192,128]{2,1,0:T(8,128)S(1)}, u32[]{:S(2)}) copy-start(f32[8,192,128]{2,1,0:T(8,128)S(1)} %fusion.128) | copy-start | bytes 2359300
  214.9 17.0 %collective-permute-start.18 = (f32[4,192,128]{2,1,0:T(8,128)}, f32[4,192,128]{2,1,0:T(8,128)S(1)}, u32[]{:S(2)}, u32[]{:S(2)}) collective-permute-start(f32[4,192,128]{2,1,0:T(8,128)} %get-tuple-element.32), channel_id=1, source_target_pairs={{4,0},{8,4},{12,8},{16,12},{20,16},{24,20},{28,24},{32,28},{36,32}... | collective-permute-start | bytes 1179656 | tf_op jit(solution)/shard_map/ppermute | solution.py:16
  217.1 21.9 %collective-permute-start.19 = (f32[4,192,128]{2,1,0:T(8,128)}, f32[4,192,128]{2,1,0:T(8,128)S(1)}, u32[]{:S(2)}, u32[]{:S(2)}) collective-permute-start(f32[4,192,128]{2,1,0:T(8,128)} %get-tuple-element.31), channel_id=1, source_target_pairs={{0,4},{4,8},{8,12},{12,16},{16,20},{20,24},{24,28},{28,32},{32,36}... | collective-permute-start | bytes 1179656 | tf_op jit(solution)/shard_map/ppermute | solution.py:15
  222.6 66.2 %collective-permute-start = (f32[4,192,128]{2,1,0:T(8,128)}, f32[4,192,128]{2,1,0:T(8,128)S(1)}, u32[]{:S(2)}, u32[]{:S(2)}) collective-permute-start(f32[4,192,128]{2,1,0:T(8,128)} %get-tuple-element.28), channel_id=1, source_target_pairs={{4,0},{8,4},{12,8},{16,12},{20,16},{24,20},{28,24},{32,28},{36,32}... | collective-permute-start | bytes 1179656 | tf_op jit(solution)/shard_map/ppermute | solution.py:16
  225.1 63.7 %collective-permute-start.1 = (f32[4,192,128]{2,1,0:T(8,128)}, f32[4,192,128]{2,1,0:T(8,128)}, u32[]{:S(2)}, u32[]{:S(2)}) collective-permute-start(f32[4,192,128]{2,1,0:T(8,128)} %get-tuple-element.27), channel_id=1, source_target_pairs={{0,4},{4,8},{8,12},{12,16},{16,20},{20,24},{24,28},{28,32},{32,36}... | collective-permute-start | bytes 1179656 | tf_op jit(solution)/shard_map/ppermute | solution.py:15
  243.2 29.5 %copy-start.15 = (f32[8,192,128]{2,1,0:T(8,128)}, f32[8,192,128]{2,1,0:T(8,128)S(1)}, u32[]{:S(2)}) copy-start(f32[8,192,128]{2,1,0:T(8,128)S(1)} %fusion.143) | copy-start | bytes 2359300
  244.4 19.4 %collective-permute-start.20 = (f32[4,192,128]{2,1,0:T(8,128)}, f32[4,192,128]{2,1,0:T(8,128)}, u32[]{:S(2)}, u32[]{:S(2)}) collective-permute-start(f32[4,192,128]{2,1,0:T(8,128)} %get-tuple-element.30), channel_id=1, source_target_pairs={{4,0},{8,4},{12,8},{16,12},{20,16},{24,20},{28,24},{32,28},{36,32}... | collective-permute-start | bytes 1179656 | tf_op jit(solution)/shard_map/ppermute | solution.py:16
  246.3 26.5 %collective-permute-start.21 = (f32[4,192,128]{2,1,0:T(8,128)}, f32[4,192,128]{2,1,0:T(8,128)}, u32[]{:S(2)}, u32[]{:S(2)}) collective-permute-start(f32[4,192,128]{2,1,0:T(8,128)} %get-tuple-element.29), channel_id=1, source_target_pairs={{0,4},{4,8},{8,12},{12,16},{16,20},{20,24},{24,28},{28,32},{32,36}... | collective-permute-start | bytes 1179656 | tf_op jit(solution)/shard_map/ppermute | solution.py:15
  301.4 47.5 %copy-start.16 = (f32[8,192,128]{2,1,0:T(8,128)}, f32[8,192,128]{2,1,0:T(8,128)S(1)}, u32[]{:S(2)}) copy-start(f32[8,192,128]{2,1,0:T(8,128)S(1)} %fusion.8) | copy-start | bytes 2359300
  302.5 15.0 %collective-permute-start.22 = (f32[4,192,128]{2,1,0:T(8,128)}, f32[4,192,128]{2,1,0:T(8,128)S(1)}, u32[]{:S(2)}, u32[]{:S(2)}) collective-permute-start(f32[4,192,128]{2,1,0:T(8,128)} %get-tuple-element.26), channel_id=1, source_target_pairs={{4,0},{8,4},{12,8},{16,12},{20,16},{24,20},{28,24},{32,28},{36,32}... | collective-permute-start | bytes 1179656 | tf_op jit(solution)/shard_map/ppermute | solution.py:16
  304.6 18.7 %collective-permute-start.23 = (f32[4,192,128]{2,1,0:T(8,128)}, f32[4,192,128]{2,1,0:T(8,128)}, u32[]{:S(2)}, u32[]{:S(2)}) collective-permute-start(f32[4,192,128]{2,1,0:T(8,128)} %get-tuple-element.25), channel_id=1, source_target_pairs={{0,4},{4,8},{8,12},{12,16},{16,20},{20,24},{24,28},{28,32},{32,36}... | collective-permute-start | bytes 1179656 | tf_op jit(solution)/shard_map/ppermute | solution.py:15
  328.0 20.9 %collective-permute-start.24 = (f32[4,192,128]{2,1,0:T(8,128)}, f32[4,192,128]{2,1,0:T(8,128)S(1)}, u32[]{:S(2)}, u32[]{:S(2)}) collective-permute-start(f32[4,192,128]{2,1,0:T(8,128)} %get-tuple-element.24), channel_id=1, source_target_pairs={{4,0},{8,4},{12,8},{16,12},{20,16},{24,20},{28,24},{32,28},{36,32}... | collective-permute-start | bytes 1179656 | tf_op jit(solution)/shard_map/ppermute | solution.py:16
  330.2 18.7 %collective-permute-start.25 = (f32[4,192,128]{2,1,0:T(8,128)}, f32[4,192,128]{2,1,0:T(8,128)}, u32[]{:S(2)}, u32[]{:S(2)}) collective-permute-start(f32[4,192,128]{2,1,0:T(8,128)} %get-tuple-element.23), channel_id=1, source_target_pairs={{0,4},{4,8},{8,12},{12,16},{16,20},{20,24},{24,28},{28,32},{32,36}... | collective-permute-start | bytes 1179656 | tf_op jit(solution)/shard_map/ppermute | solution.py:15
  353.2 15.0 %collective-permute-start.26 = (f32[4,192,128]{2,1,0:T(8,128)}, f32[4,192,128]{2,1,0:T(8,128)S(1)}, u32[]{:S(2)}, u32[]{:S(2)}) collective-permute-start(f32[4,192,128]{2,1,0:T(8,128)} %get-tuple-element.22), channel_id=1, source_target_pairs={{4,0},{8,4},{12,8},{16,12},{20,16},{24,20},{28,24},{32,28},{36,32}... | collective-permute-start | bytes 1179656 | tf_op jit(solution)/shard_map/ppermute | solution.py:16
  355.3 18.6 %collective-permute-start.27 = (f32[4,192,128]{2,1,0:T(8,128)S(1)}, f32[4,192,128]{2,1,0:T(8,128)S(1)}, u32[]{:S(2)}, u32[]{:S(2)}) collective-permute-start(f32[4,192,128]{2,1,0:T(8,128)S(1)} %get-tuple-element.21), channel_id=1, source_target_pairs={{0,4},{4,8},{8,12},{12,16},{16,20},{20,24},{24,28},{28,32},{32,36}... | collective-permute-start | bytes 1179656 | tf_op jit(solution)/shard_map/ppermute | solution.py:15
  378.1 50.0 %copy-start.21 = (f32[8,192,128]{2,1,0:T(8,128)}, f32[8,192,128]{2,1,0:T(8,128)S(1)}, u32[]{:S(2)}) copy-start(f32[8,192,128]{2,1,0:T(8,128)S(1)} %fusion.203) | copy-start | bytes 2359300
  379.0 21.5 %collective-permute-start.28 = (f32[4,192,128]{2,1,0:T(8,128)}, f32[4,192,128]{2,1,0:T(8,128)S(1)}, u32[]{:S(2)}, u32[]{:S(2)}) collective-permute-start(f32[4,192,128]{2,1,0:T(8,128)} %get-tuple-element.20), channel_id=1, source_target_pairs={{4,0},{8,4},{12,8},{16,12},{20,16},{24,20},{28,24},{32,28},{36,32}... | collective-permute-start | bytes 1179656 | tf_op jit(solution)/shard_map/ppermute | solution.py:16
  381.2 20.2 %collective-permute-start.29 = (f32[4,192,128]{2,1,0:T(8,128)}, f32[4,192,128]{2,1,0:T(8,128)}, u32[]{:S(2)}, u32[]{:S(2)}) collective-permute-start(f32[4,192,128]{2,1,0:T(8,128)} %get-tuple-element.19), channel_id=1, source_target_pairs={{0,4},{4,8},{8,12},{12,16},{16,20},{20,24},{24,28},{28,32},{32,36}... | collective-permute-start | bytes 1179656 | tf_op jit(solution)/shard_map/ppermute | solution.py:15
  405.9 15.0 %collective-permute-start.30 = (f32[4,192,128]{2,1,0:T(8,128)}, f32[4,192,128]{2,1,0:T(8,128)S(1)}, u32[]{:S(2)}, u32[]{:S(2)}) collective-permute-start(f32[4,192,128]{2,1,0:T(8,128)} %get-tuple-element.18), channel_id=1, source_target_pairs={{4,0},{8,4},{12,8},{16,12},{20,16},{24,20},{28,24},{32,28},{36,32}... | collective-permute-start | bytes 1179656 | tf_op jit(solution)/shard_map/ppermute | solution.py:16
  408.1 19.9 %collective-permute-start.31 = (f32[4,192,128]{2,1,0:T(8,128)}, f32[4,192,128]{2,1,0:T(8,128)}, u32[]{:S(2)}, u32[]{:S(2)}) collective-permute-start(f32[4,192,128]{2,1,0:T(8,128)} %get-tuple-element.17), channel_id=1, source_target_pairs={{0,4},{4,8},{8,12},{12,16},{16,20},{20,24},{24,28},{28,32},{32,36}... | collective-permute-start | bytes 1179656 | tf_op jit(solution)/shard_map/ppermute | solution.py:15
  432.6 20.9 %collective-permute-start.32 = (f32[4,192,128]{2,1,0:T(8,128)}, f32[4,192,128]{2,1,0:T(8,128)S(1)}, u32[]{:S(2)}, u32[]{:S(2)}) collective-permute-start(f32[4,192,128]{2,1,0:T(8,128)} %get-tuple-element.16), channel_id=1, source_target_pairs={{4,0},{8,4},{12,8},{16,12},{20,16},{24,20},{28,24},{32,28},{36,32}... | collective-permute-start | bytes 1179656 | tf_op jit(solution)/shard_map/ppermute | solution.py:16
  434.8 20.8 %collective-permute-start.33 = (f32[4,192,128]{2,1,0:T(8,128)}, f32[4,192,128]{2,1,0:T(8,128)}, u32[]{:S(2)}, u32[]{:S(2)}) collective-permute-start(f32[4,192,128]{2,1,0:T(8,128)} %get-tuple-element.15), channel_id=1, source_target_pairs={{0,4},{4,8},{8,12},{12,16},{16,20},{20,24},{24,28},{28,32},{32,36}... | collective-permute-start | bytes 1179656 | tf_op jit(solution)/shard_map/ppermute | solution.py:15
  460.2 15.2 %collective-permute-start.34 = (f32[4,192,128]{2,1,0:T(8,128)}, f32[4,192,128]{2,1,0:T(8,128)S(1)}, u32[]{:S(2)}, u32[]{:S(2)}) collective-permute-start(f32[4,192,128]{2,1,0:T(8,128)} %get-tuple-element.14), channel_id=1, source_target_pairs={{4,0},{8,4},{12,8},{16,12},{20,16},{24,20},{28,24},{32,28},{36,32}... | collective-permute-start | bytes 1179656 | tf_op jit(solution)/shard_map/ppermute | solution.py:16
  462.6 19.5 %collective-permute-start.35 = (f32[4,192,128]{2,1,0:T(8,128)}, f32[4,192,128]{2,1,0:T(8,128)}, u32[]{:S(2)}, u32[]{:S(2)}) collective-permute-start(f32[4,192,128]{2,1,0:T(8,128)} %get-tuple-element.13), channel_id=1, source_target_pairs={{0,4},{4,8},{8,12},{12,16},{16,20},{20,24},{24,28},{28,32},{32,36}... | collective-permute-start | bytes 1179656 | tf_op jit(solution)/shard_map/ppermute | solution.py:15
  486.6 20.0 %collective-permute-start.36 = (f32[4,192,128]{2,1,0:T(8,128)}, f32[4,192,128]{2,1,0:T(8,128)S(1)}, u32[]{:S(2)}, u32[]{:S(2)}) collective-permute-start(f32[4,192,128]{2,1,0:T(8,128)} %get-tuple-element.12), channel_id=1, source_target_pairs={{4,0},{8,4},{12,8},{16,12},{20,16},{24,20},{28,24},{32,28},{36,32}... | collective-permute-start | bytes 1179656 | tf_op jit(solution)/shard_map/ppermute | solution.py:16
  488.8 20.3 %collective-permute-start.37 = (f32[4,192,128]{2,1,0:T(8,128)}, f32[4,192,128]{2,1,0:T(8,128)}, u32[]{:S(2)}, u32[]{:S(2)}) collective-permute-start(f32[4,192,128]{2,1,0:T(8,128)} %get-tuple-element.11), channel_id=1, source_target_pairs={{0,4},{4,8},{8,12},{12,16},{16,20},{20,24},{24,28},{28,32},{32,36}... | collective-permute-start | bytes 1179656 | tf_op jit(solution)/shard_map/ppermute | solution.py:15
  523.5 15.1 %collective-permute-start.38 = (f32[4,192,128]{2,1,0:T(8,128)}, f32[4,192,128]{2,1,0:T(8,128)}, u32[]{:S(2)}, u32[]{:S(2)}) collective-permute-start(f32[4,192,128]{2,1,0:T(8,128)} %get-tuple-element.10), channel_id=1, source_target_pairs={{4,0},{8,4},{12,8},{16,12},{20,16},{24,20},{28,24},{32,28},{36,32}... | collective-permute-start | bytes 1179656 | tf_op jit(solution)/shard_map/ppermute | solution.py:16
  525.7 18.7 %collective-permute-start.39 = (f32[4,192,128]{2,1,0:T(8,128)S(1)}, f32[4,192,128]{2,1,0:T(8,128)}, u32[]{:S(2)}, u32[]{:S(2)}) collective-permute-start(f32[4,192,128]{2,1,0:T(8,128)S(1)} %get-tuple-element.9), channel_id=1, source_target_pairs={{0,4},{4,8},{8,12},{12,16},{16,20},{20,24},{24,28},{28,32},{32,36}... | collective-permute-start | bytes 1179656 | tf_op jit(solution)/shard_map/ppermute | solution.py:15
  560.7 3.6 collective-permute-start.40
  564.4 10.3 %collective-permute-start.41 = (f32[8,48,128]{2,1,0:T(8,128)S(1)}, f32[8,48,128]{2,1,0:T(8,128)S(1)}, u32[]{:S(2)}, u32[]{:S(2)}) collective-permute-start(f32[8,48,128]{2,1,0:T(8,128)S(1)} %dynamic-slice_bitcast_fusion), channel_id=1, source_target_pairs={{0,2},{1,3},{2,0},{3,1},{4,6},{5,7},{6,4},{7,5},{8,10},{9,11},{10,... | collective-permute-start | bytes 589832 | tf_op jit(solution)/shard_map/ppermute | solution.py:121
  (45 other events, 395.9 us)

commit v2 on v1

--- a/solution.py
+++ b/solution.py
@@ -1,6 +1,8 @@
 import jax
 import jax.numpy as jnp
 from jax import lax
+from jax.experimental import pallas as pl
+from jax.experimental.pallas import tpu as pltpu
 from jax.sharding import PartitionSpec as P
 
 TAPS = (-205.0 / 72.0, 8.0 / 5.0, -1.0 / 5.0, 8.0 / 315.0, -1.0 / 560.0)
@@ -54,11 +56,41 @@
     return result
 
 
+def update_kernel(current, former, courant_sq, interior, low, high, injected, latest):
+    length_x = current.shape[0]
+    for plane in range(length_x):
+        edge = None
+        for distance in range(1, 5):
+            for near in (plane - distance, plane + distance):
+                if near < 0:
+                    term = low[near + RADIUS]
+                elif near >= length_x:
+                    term = high[near - length_x]
+                else:
+                    continue
+                term = TAPS[distance] * term
+                edge = term if edge is None else edge + term
+        lap = interior[plane] if edge is None else interior[plane] + edge
+        latest[plane] = (
+            2.0 * current[plane] - former[plane] + courant_sq[plane] * lap + injected[plane]
+        )
+
+
+def fused_update(current, former, courant_sq, interior, low, high, injected):
+    cells = current.size
+    return pl.pallas_call(
+        update_kernel,
+        out_shape=jax.ShapeDtypeStruct(current.shape, current.dtype),
+        in_specs=[pl.BlockSpec(memory_space=pltpu.VMEM)] * 7,
+        out_specs=pl.BlockSpec(memory_space=pltpu.VMEM),
+        cost_estimate=pl.CostEstimate(flops=12 * cells, transcendentals=0, bytes_accessed=28 * cells),
+    )(current, former, courant_sq, interior, low, high, injected)
+
+
 def step(current, former, courant_sq, injected):
     low, high = exchange_edges(current)
     interior = inner_laplace(current)
-    lap = interior + edge_terms(low, high, current.shape[0])
-    return 2.0 * current - former + courant_sq * lap + injected
+    return fused_update(current, former, courant_sq, interior, low, high, injected)
 
 
 def per_device(

time: 586 us -> 594 us (1.014)
  the two profiles are of different devices: /device:TPU:46 before, /device:TPU:388 now
where the time goes in v2:
time: 594 us; the launch traced here: 583 us
  starting transfers between devices  208 us (35%)
  other arithmetic  173 us (29%)
  local copies, waits for them, and re-layouts  77.7 us (13%)
  Pallas kernels  69.8 us (12%)
  waiting for transfers between devices  51.8 us (9%)
    ppermute x20, starting transfers between devices, exchange_edges(): high = lax.ppermute(block[:RADIUS], 'space', backward)  151 us
    add x20, other arithmetic, inner_laplace(): result = result + TAPS[distance] * beside_all  90.6 us
    pallas_call x20, Pallas kernels, fused_update(): pl.pallas_call(update_kernel, out_shape=jax.ShapeDtypeStruct(current.shap...  69.8 us
    ppermute x20, starting transfers between devices, exchange_edges(): low = lax.ppermute(block[block.shape[0] - RADIUS:], 'space', forward)  53.2 us
    scatter-add x10, other arithmetic, per_device(): injected = empty_flat.at[receiver_cells].add(misfit[t])  43.8 us
    gather x10, local copies, waits for them, and re-layouts, per_device(): traces.append(latest.reshape(-1)[receiver_cells])  38.9 us
    ppermute x20, waiting for transfers between devices, exchange_edges(): high = lax.ppermute(block[:RADIUS], 'space', backward)  27.2 us
    slice x20, local copies, waits for them, and re-layouts, exchange_edges(): high = lax.ppermute(block[:RADIUS], 'space', backward)  25 us
  transfers between devices with their start and end apart: 42, of which 18 were waited for; matrix products, arithmetic and copies ran while one was open for 36% of the time, Pallas kernels for 3%

profile of v2, /device:TPU:388, one launch (start us, length us, event | category | flops | bytes accessed | tf_op | source)
XLA Modules:
  0.0 582.9 jit_solution(2799954967201494518)
XLA Ops:
  4.4 7.0 %collective-permute-start.3 = (f32[4,192,128]{2,1,0:T(8,128)S(1)}, f32[4,192,128]{2,1,0:T(8,128)S(1)}, u32[]{:S(2)}, u32[]{:S(2)}) collective-permute-start(f32[4,192,128]{2,1,0:T(8,128)S(1)} %get-tuple-element.43), channel_id=1, source_target_pairs={{4,0},{8,4},{12,8},{16,12},{20,16},{24,20},{28,24},{32,28},{36,32}... | collective-permute-start | bytes 1179656 | tf_op jit(solution)/shard_map/ppermute | solution.py:18
  32.1 7.0 %collective-permute-start.5 = (f32[4,192,128]{2,1,0:T(8,128)S(1)}, f32[4,192,128]{2,1,0:T(8,128)S(1)}, u32[]{:S(2)}, u32[]{:S(2)}) collective-permute-start(f32[4,192,128]{2,1,0:T(8,128)S(1)} %get-tuple-element.41), channel_id=1, source_target_pairs={{4,0},{8,4},{12,8},{16,12},{20,16},{24,20},{28,24},{32,28},{36,32}... | collective-permute-start | bytes 1179656 | tf_op jit(solution)/shard_map/ppermute | solution.py:18
  59.0 7.0 %collective-permute-start.7 = (f32[4,192,128]{2,1,0:T(8,128)S(1)}, f32[4,192,128]{2,1,0:T(8,128)S(1)}, u32[]{:S(2)}, u32[]{:S(2)}) collective-permute-start(f32[4,192,128]{2,1,0:T(8,128)S(1)} %get-tuple-element.39), channel_id=1, source_target_pairs={{4,0},{8,4},{12,8},{16,12},{20,16},{24,20},{28,24},{32,28},{36,32}... | collective-permute-start | bytes 1179656 | tf_op jit(solution)/shard_map/ppermute | solution.py:18
  84.6 7.0 %collective-permute-start.9 = (f32[4,192,128]{2,1,0:T(8,128)S(1)}, f32[4,192,128]{2,1,0:T(8,128)S(1)}, u32[]{:S(2)}, u32[]{:S(2)}) collective-permute-start(f32[4,192,128]{2,1,0:T(8,128)S(1)} %get-tuple-element.37), channel_id=1, source_target_pairs={{4,0},{8,4},{12,8},{16,12},{20,16},{24,20},{28,24},{32,28},{36,32}... | collective-permute-start | bytes 1179656 | tf_op jit(solution)/shard_map/ppermute | solution.py:18
  98.7 6.4 %collective-permute-done.9.high = f32[4,192,128]{2,1,0:T(8,128)S(1)} collective-permute-done((f32[4,192,128]{2,1,0:T(8,128)S(1)}, f32[4,192,128]{2,1,0:T(8,128)S(1)}, u32[]{:S(2)}, u32[]{:S(2)}) %collective-permute-start.9) | collective-permute-done | bytes 393248 | tf_op jit(solution)/shard_map/ppermute | solution.py:18
  113.5 7.2 %collective-permute-start.11 = (f32[4,192,128]{2,1,0:T(8,128)S(1)}, f32[4,192,128]{2,1,0:T(8,128)S(1)}, u32[]{:S(2)}, u32[]{:S(2)}) collective-permute-start(f32[4,192,128]{2,1,0:T(8,128)S(1)} %get-tuple-element.35), channel_id=1, source_target_pairs={{4,0},{8,4},{12,8},{16,12},{20,16},{24,20},{28,24},{32,28},{36,32}... | collective-permute-start | bytes 1179656 | tf_op jit(solution)/shard_map/ppermute | solution.py:18
  128.1 3.9 collective-permute-done.11.high
  140.4 7.2 %collective-permute-start.13 = (f32[4,192,128]{2,1,0:T(8,128)S(1)}, f32[4,192,128]{2,1,0:T(8,128)}, u32[]{:S(2)}, u32[]{:S(2)}) collective-permute-start(f32[4,192,128]{2,1,0:T(8,128)S(1)} %get-tuple-element.33), channel_id=1, source_target_pairs={{4,0},{8,4},{12,8},{16,12},{20,16},{24,20},{28,24},{32,28},{36,32}... | collective-permute-start | bytes 1179656 | tf_op jit(solution)/shard_map/ppermute | solution.py:18
  149.7 8.1 %collective-permute-start.1 = (f32[4,192,128]{2,1,0:T(8,128)S(1)}, f32[4,192,128]{2,1,0:T(8,128)}, u32[]{:S(2)}, u32[]{:S(2)}) collective-permute-start(f32[4,192,128]{2,1,0:T(8,128)S(1)} %get-tuple-element.45), channel_id=1, source_target_pairs={{4,0},{8,4},{12,8},{16,12},{20,16},{24,20},{28,24},{32,28},{36,32}... | collective-permute-start | bytes 1179656 | tf_op jit(solution)/shard_map/ppermute | solution.py:18
  171.0 4.5 collective-permute-start.14
  175.5 5.6 collective-permute-start.15
  191.7 3.5 shard_map.106.current.former
  199.4 7.2 %collective-permute-start.17 = (f32[4,192,128]{2,1,0:T(8,128)S(1)}, f32[4,192,128]{2,1,0:T(8,128)S(1)}, u32[]{:S(2)}, u32[]{:S(2)}) collective-permute-start(f32[4,192,128]{2,1,0:T(8,128)S(1)} %get-tuple-element.29), channel_id=1, source_target_pairs={{4,0},{8,4},{12,8},{16,12},{20,16},{24,20},{28,24},{32,28},{36,32}... | collective-permute-start | bytes 1179656 | tf_op jit(solution)/shard_map/ppermute | solution.py:18
  224.6 7.6 %collective-permute-start.19 = (f32[4,192,128]{2,1,0:T(8,128)S(1)}, f32[4,192,128]{2,1,0:T(8,128)S(1)}, u32[]{:S(2)}, u32[]{:S(2)}) collective-permute-start(f32[4,192,128]{2,1,0:T(8,128)S(1)} %get-tuple-element.27), channel_id=1, source_target_pairs={{4,0},{8,4},{12,8},{16,12},{20,16},{24,20},{28,24},{32,28},{36,32}... | collective-permute-start | bytes 1179656 | tf_op jit(solution)/shard_map/ppermute | solution.py:18
  239.2 6.5 %collective-permute-done.19.high = f32[4,192,128]{2,1,0:T(8,128)S(1)} collective-permute-done((f32[4,192,128]{2,1,0:T(8,128)S(1)}, f32[4,192,128]{2,1,0:T(8,128)S(1)}, u32[]{:S(2)}, u32[]{:S(2)}) %collective-permute-start.19) | collective-permute-done | bytes 393248 | tf_op jit(solution)/shard_map/ppermute | solution.py:18
  254.1 7.2 %collective-permute-start.21 = (f32[4,192,128]{2,1,0:T(8,128)S(1)}, f32[4,192,128]{2,1,0:T(8,128)S(1)}, u32[]{:S(2)}, u32[]{:S(2)}) collective-permute-start(f32[4,192,128]{2,1,0:T(8,128)S(1)} %get-tuple-element.25), channel_id=1, source_target_pairs={{4,0},{8,4},{12,8},{16,12},{20,16},{24,20},{28,24},{32,28},{36,32}... | collective-permute-start | bytes 1179656 | tf_op jit(solution)/shard_map/ppermute | solution.py:18
  267.8 4.2 gather_fusion.1
  272.9 3.5 shard_map.109
  276.5 6.3 %gather_fusion = f32[512]{0:T(512)S(1)} fusion(f32[196608]{0:T(1024)} %bitcast.122, s32[1024]{0:T(1024)S(1)} %pad_clamp_fusion), kind=kCustom, calls=%fused_computation | custom fusion | bytes 6144 | tf_op jit(solution)/shard_map/gather | solution.py:126
  283.3 4.3 scatter_custom_fusion.10
  295.9 7.3 %collective-permute-start.23 = (f32[4,192,128]{2,1,0:T(8,128)S(1)}, f32[4,192,128]{2,1,0:T(8,128)S(1)}, u32[]{:S(2)}, u32[]{:S(2)}) collective-permute-start(f32[4,192,128]{2,1,0:T(8,128)S(1)} %get-tuple-element.23), channel_id=1, source_target_pairs={{4,0},{8,4},{12,8},{16,12},{20,16},{24,20},{28,24},{32,28},{36,32}... | collective-permute-start | bytes 1179656 | tf_op jit(solution)/shard_map/ppermute | solution.py:18
  309.6 4.5 scatter_custom_fusion.11
  325.0 8.3 %collective-permute-start.25 = (f32[4,192,128]{2,1,0:T(8,128)S(1)}, f32[4,192,128]{2,1,0:T(8,128)S(1)}, u32[]{:S(2)}, u32[]{:S(2)}) collective-permute-start(f32[4,192,128]{2,1,0:T(8,128)S(1)} %get-tuple-element.21), channel_id=1, source_target_pairs={{4,0},{8,4},{12,8},{16,12},{20,16},{24,20},{28,24},{32,28},{36,32}... | collective-permute-start | bytes 1179656 | tf_op jit(solution)/shard_map/ppermute | solution.py:18
  333.4 4.4 scatter_custom_fusion.12
  348.9 7.8 %collective-permute-start.27 = (f32[4,192,128]{2,1,0:T(8,128)S(1)}, f32[4,192,128]{2,1,0:T(8,128)S(1)}, u32[]{:S(2)}, u32[]{:S(2)}) collective-permute-start(f32[4,192,128]{2,1,0:T(8,128)S(1)} %get-tuple-element.19), channel_id=1, source_target_pairs={{4,0},{8,4},{12,8},{16,12},{20,16},{24,20},{28,24},{32,28},{36,32}... | collective-permute-start | bytes 1179656 | tf_op jit(solution)/shard_map/ppermute | solution.py:18
  363.1 4.5 scatter_custom_fusion.13
  378.5 8.1 %collective-permute-start.29 = (f32[4,192,128]{2,1,0:T(8,128)S(1)}, f32[4,192,128]{2,1,0:T(8,128)S(1)}, u32[]{:S(2)}, u32[]{:S(2)}) collective-permute-start(f32[4,192,128]{2,1,0:T(8,128)S(1)} %get-tuple-element.17), channel_id=1, source_target_pairs={{4,0},{8,4},{12,8},{16,12},{20,16},{24,20},{28,24},{32,28},{36,32}... | collective-permute-start | bytes 1179656 | tf_op jit(solution)/shard_map/ppermute | solution.py:18
  387.2 4.3 scatter_custom_fusion.14
  395.7 3.5 shard_map.114.current.former
  402.7 8.1 %collective-permute-start.31 = (f32[4,192,128]{2,1,0:T(8,128)S(1)}, f32[4,192,128]{2,1,0:T(8,128)}, u32[]{:S(2)}, u32[]{:S(2)}) collective-permute-start(f32[4,192,128]{2,1,0:T(8,128)S(1)} %get-tuple-element.15), channel_id=1, source_target_pairs={{4,0},{8,4},{12,8},{16,12},{20,16},{24,20},{28,24},{32,28},{36,32}... | collective-permute-start | bytes 1179656 | tf_op jit(solution)/shard_map/ppermute | solution.py:18
  410.8 4.2 gather_fusion.7
  415.0 4.2 gather_fusion.6
  419.2 4.5 scatter_custom_fusion.15
  434.5 8.1 %collective-permute-start.33 = (f32[4,192,128]{2,1,0:T(8,128)S(1)}, f32[4,192,128]{2,1,0:T(8,128)}, u32[]{:S(2)}, u32[]{:S(2)}) collective-permute-start(f32[4,192,128]{2,1,0:T(8,128)S(1)} %get-tuple-element.13), channel_id=1, source_target_pairs={{4,0},{8,4},{12,8},{16,12},{20,16},{24,20},{28,24},{32,28},{36,32}... | collective-permute-start | bytes 1179656 | tf_op jit(solution)/shard_map/ppermute | solution.py:18
  443.2 4.3 scatter_custom_fusion.16
  459.0 8.1 %collective-permute-start.35 = (f32[4,192,128]{2,1,0:T(8,128)S(1)}, f32[4,192,128]{2,1,0:T(8,128)}, u32[]{:S(2)}, u32[]{:S(2)}) collective-permute-start(f32[4,192,128]{2,1,0:T(8,128)S(1)} %get-tuple-element.11), channel_id=1, source_target_pairs={{4,0},{8,4},{12,8},{16,12},{20,16},{24,20},{28,24},{32,28},{36,32}... | collective-permute-start | bytes 1179656 | tf_op jit(solution)/shard_map/ppermute | solution.py:18
  470.4 4.3 gather_fusion.8
  474.6 4.3 scatter_custom_fusion.17
  479.0 11.9 %fusion.485.interior = f32[8,192,128]{2,1,0:T(8,128)} fusion(f32[8,192,128]{2,1,0:T(8,128)} %shard_map.116.current.former), kind=kLoop, calls=%fused_computation.995 | loop fusion | flops 5701632 | bytes 1572864 | tf_op jit(solution)/shard_map/add | solution.py:41
  490.9 3.5 shard_map.117.current.former
  498.2 8.4 %collective-permute-start.37 = (f32[4,192,128]{2,1,0:T(8,128)S(1)}, f32[4,192,128]{2,1,0:T(8,128)}, u32[]{:S(2)}, u32[]{:S(2)}) collective-permute-start(f32[4,192,128]{2,1,0:T(8,128)S(1)} %get-tuple-element.9), channel_id=1, source_target_pairs={{4,0},{8,4},{12,8},{16,12},{20,16},{24,20},{28,24},{32,28},{36,32}... | collective-permute-start | bytes 1179656 | tf_op jit(solution)/shard_map/ppermute | solution.py:18
  507.3 4.3 scatter_custom_fusion.18
  511.6 11.5 %fusion.513.interior = f32[8,192,128]{2,1,0:T(8,128)} fusion(f32[8,192,128]{2,1,0:T(8,128)} %shard_map.117.current.former), kind=kLoop, calls=%fused_computation.1023 | loop fusion | flops 5701632 | bytes 1572864 | tf_op jit(solution)/shard_map/add | solution.py:41
  530.4 8.1 %collective-permute-start.39 = (f32[4,192,128]{2,1,0:T(8,128)S(1)}, f32[4,192,128]{2,1,0:T(8,128)}, u32[]{:S(2)}, u32[]{:S(2)}) collective-permute-start(f32[4,192,128]{2,1,0:T(8,128)S(1)} %get-tuple-element.7), channel_id=1, source_target_pairs={{4,0},{8,4},{12,8},{16,12},{20,16},{24,20},{28,24},{32,28},{36,32}... | collective-permute-start | bytes 1179656 | tf_op jit(solution)/shard_map/ppermute | solution.py:18
  538.6 4.3 scatter_custom_fusion.19
  542.9 11.4 %fusion.541.interior = f32[8,192,128]{2,1,0:T(8,128)} fusion(f32[8,192,128]{2,1,0:T(8,128)} %shard_map.118.current), kind=kLoop, calls=%fused_computation.1051 | loop fusion | flops 5701632 | bytes 1572864 | tf_op jit(solution)/shard_map/add | solution.py:41
  557.8 7.0 %multiply_add_fusion = f32[8,192,128]{2,1,0:T(8,128)S(1)} fusion(f32[8,192,128]{2,1,0:T(8,128)} %shard_map.119, f32[8,192,128]{2,1,0:T(8,128)S(1)} %copy-done.1, f32[8,192,128]{2,1,0:T(8,128)} %shard_map.118.current, f32[8,192,128]{2,1,0:T(8,128)S(1)} %copy-done.3, f32[8,192,128]{2,1,0:T(8,128)} %shard_map.117.current.former, ...), kind=kLoop, calls=%fused_computation.1070 | loop fusion | flops 9633792 | bytes 18087936 | tf_op jit(solution)/shard_map/add | solution.py:139
  572.9 7.9 %collective-permute-done.41 = f32[8,48,128]{2,1,0:T(8,128)S(1)} collective-permute-done((f32[8,48,128]{2,1,0:T(8,128)S(1)}, f32[8,48,128]{2,1,0:T(8,128)S(1)}, u32[]{:S(2)}, u32[]{:S(2)}) %collective-permute-start.41) | collective-permute-done | bytes 196640 | tf_op jit(solution)/shard_map/ppermute | solution.py:153
  (285 shorter events, 278.2 us)
Async XLA Ops:
  1.3 19.9 %collective-permute-start.2 = (f32[4,192,128]{2,1,0:T(8,128)S(1)}, f32[4,192,128]{2,1,0:T(8,128)S(1)}, u32[]{:S(2)}, u32[]{:S(2)}) collective-permute-start(f32[4,192,128]{2,1,0:T(8,128)S(1)} %get-tuple-element.44), channel_id=1, source_target_pairs={{0,4},{4,8},{8,12},{12,16},{16,20},{20,24},{24,28},{28,32},{32,36}... | collective-permute-start | bytes 1179656 | tf_op jit(solution)/shard_map/ppermute | solution.py:17
  4.4 19.1 %collective-permute-start.3 = (f32[4,192,128]{2,1,0:T(8,128)S(1)}, f32[4,192,128]{2,1,0:T(8,128)S(1)}, u32[]{:S(2)}, u32[]{:S(2)}) collective-permute-start(f32[4,192,128]{2,1,0:T(8,128)S(1)} %get-tuple-element.43), channel_id=1, source_target_pairs={{4,0},{8,4},{12,8},{16,12},{20,16},{24,20},{28,24},{32,28},{36,32}... | collective-permute-start | bytes 1179656 | tf_op jit(solution)/shard_map/ppermute | solution.py:18
  13.4 171.0 %copy-start.70 = (s32[128]{0:T(128)}, s32[128]{0:T(128)S(1)}, u32[]{:S(2)}) copy-start(s32[128]{0:T(128)S(1)} %fusion.602) | copy-start | bytes 1540
  28.9 19.2 %collective-permute-start.4 = (f32[4,192,128]{2,1,0:T(8,128)S(1)}, f32[4,192,128]{2,1,0:T(8,128)S(1)}, u32[]{:S(2)}, u32[]{:S(2)}) collective-permute-start(f32[4,192,128]{2,1,0:T(8,128)S(1)} %get-tuple-element.42), channel_id=1, source_target_pairs={{0,4},{4,8},{8,12},{12,16},{16,20},{20,24},{24,28},{28,32},{32,36}... | collective-permute-start | bytes 1179656 | tf_op jit(solution)/shard_map/ppermute | solution.py:17
  32.1 18.2 %collective-permute-start.5 = (f32[4,192,128]{2,1,0:T(8,128)S(1)}, f32[4,192,128]{2,1,0:T(8,128)S(1)}, u32[]{:S(2)}, u32[]{:S(2)}) collective-permute-start(f32[4,192,128]{2,1,0:T(8,128)S(1)} %get-tuple-element.41), channel_id=1, source_target_pairs={{4,0},{8,4},{12,8},{16,12},{20,16},{24,20},{28,24},{32,28},{36,32}... | collective-permute-start | bytes 1179656 | tf_op jit(solution)/shard_map/ppermute | solution.py:18
  55.7 18.2 %collective-permute-start.6 = (f32[4,192,128]{2,1,0:T(8,128)S(1)}, f32[4,192,128]{2,1,0:T(8,128)S(1)}, u32[]{:S(2)}, u32[]{:S(2)}) collective-permute-start(f32[4,192,128]{2,1,0:T(8,128)S(1)} %get-tuple-element.40), channel_id=1, source_target_pairs={{0,4},{4,8},{8,12},{12,16},{16,20},{20,24},{24,28},{28,32},{32,36}... | collective-permute-start | bytes 1179656 | tf_op jit(solution)/shard_map/ppermute | solution.py:17
  59.0 17.0 %collective-permute-start.7 = (f32[4,192,128]{2,1,0:T(8,128)S(1)}, f32[4,192,128]{2,1,0:T(8,128)S(1)}, u32[]{:S(2)}, u32[]{:S(2)}) collective-permute-start(f32[4,192,128]{2,1,0:T(8,128)S(1)} %get-tuple-element.39), channel_id=1, source_target_pairs={{4,0},{8,4},{12,8},{16,12},{20,16},{24,20},{28,24},{32,28},{36,32}... | collective-permute-start | bytes 1179656 | tf_op jit(solution)/shard_map/ppermute | solution.py:18
  81.4 17.3 %collective-permute-start.8 = (f32[4,192,128]{2,1,0:T(8,128)S(1)}, f32[4,192,128]{2,1,0:T(8,128)S(1)}, u32[]{:S(2)}, u32[]{:S(2)}) collective-permute-start(f32[4,192,128]{2,1,0:T(8,128)S(1)} %get-tuple-element.38), channel_id=1, source_target_pairs={{0,4},{4,8},{8,12},{12,16},{16,20},{20,24},{24,28},{28,32},{32,36}... | collective-permute-start | bytes 1179656 | tf_op jit(solution)/shard_map/ppermute | solution.py:17
  84.6 20.4 %collective-permute-start.9 = (f32[4,192,128]{2,1,0:T(8,128)S(1)}, f32[4,192,128]{2,1,0:T(8,128)S(1)}, u32[]{:S(2)}, u32[]{:S(2)}) collective-permute-start(f32[4,192,128]{2,1,0:T(8,128)S(1)} %get-tuple-element.37), channel_id=1, source_target_pairs={{4,0},{8,4},{12,8},{16,12},{20,16},{24,20},{28,24},{32,28},{36,32}... | collective-permute-start | bytes 1179656 | tf_op jit(solution)/shard_map/ppermute | solution.py:18
  110.5 17.6 %collective-permute-start.10 = (f32[4,192,128]{2,1,0:T(8,128)S(1)}, f32[4,192,128]{2,1,0:T(8,128)S(1)}, u32[]{:S(2)}, u32[]{:S(2)}) collective-permute-start(f32[4,192,128]{2,1,0:T(8,128)S(1)} %get-tuple-element.36), channel_id=1, source_target_pairs={{0,4},{4,8},{8,12},{12,16},{16,20},{20,24},{24,28},{28,32},{32,36}... | collective-permute-start | bytes 1179656 | tf_op jit(solution)/shard_map/ppermute | solution.py:17
  113.5 18.5 %collective-permute-start.11 = (f32[4,192,128]{2,1,0:T(8,128)S(1)}, f32[4,192,128]{2,1,0:T(8,128)S(1)}, u32[]{:S(2)}, u32[]{:S(2)}) collective-permute-start(f32[4,192,128]{2,1,0:T(8,128)S(1)} %get-tuple-element.35), channel_id=1, source_target_pairs={{4,0},{8,4},{12,8},{16,12},{20,16},{24,20},{28,24},{32,28},{36,32}... | collective-permute-start | bytes 1179656 | tf_op jit(solution)/shard_map/ppermute | solution.py:18
  137.5 28.8 %collective-permute-start.12 = (f32[4,192,128]{2,1,0:T(8,128)S(1)}, f32[4,192,128]{2,1,0:T(8,128)}, u32[]{:S(2)}, u32[]{:S(2)}) collective-permute-start(f32[4,192,128]{2,1,0:T(8,128)S(1)} %get-tuple-element.34), channel_id=1, source_target_pairs={{0,4},{4,8},{8,12},{12,16},{16,20},{20,24},{24,28},{28,32},{32,36}... | collective-permute-start | bytes 1179656 | tf_op jit(solution)/shard_map/ppermute | solution.py:17
  140.4 26.0 %collective-permute-start.13 = (f32[4,192,128]{2,1,0:T(8,128)S(1)}, f32[4,192,128]{2,1,0:T(8,128)}, u32[]{:S(2)}, u32[]{:S(2)}) collective-permute-start(f32[4,192,128]{2,1,0:T(8,128)S(1)} %get-tuple-element.33), channel_id=1, source_target_pairs={{4,0},{8,4},{12,8},{16,12},{20,16},{24,20},{28,24},{32,28},{36,32}... | collective-permute-start | bytes 1179656 | tf_op jit(solution)/shard_map/ppermute | solution.py:18
  147.7 140.0 %collective-permute-start = (f32[4,192,128]{2,1,0:T(8,128)S(1)}, f32[4,192,128]{2,1,0:T(8,128)S(1)}, u32[]{:S(2)}, u32[]{:S(2)}) collective-permute-start(f32[4,192,128]{2,1,0:T(8,128)S(1)} %get-tuple-element.46), channel_id=1, source_target_pairs={{0,4},{4,8},{8,12},{12,16},{16,20},{20,24},{24,28},{28,32},{32,36}... | collective-permute-start | bytes 1179656 | tf_op jit(solution)/shard_map/ppermute | solution.py:17
  149.7 137.9 %collective-permute-start.1 = (f32[4,192,128]{2,1,0:T(8,128)S(1)}, f32[4,192,128]{2,1,0:T(8,128)}, u32[]{:S(2)}, u32[]{:S(2)}) collective-permute-start(f32[4,192,128]{2,1,0:T(8,128)S(1)} %get-tuple-element.45), channel_id=1, source_target_pairs={{4,0},{8,4},{12,8},{16,12},{20,16},{24,20},{28,24},{32,28},{36,32}... | collective-permute-start | bytes 1179656 | tf_op jit(solution)/shard_map/ppermute | solution.py:18
  171.0 19.1 %collective-permute-start.14 = (f32[4,192,128]{2,1,0:T(8,128)S(1)}, f32[4,192,128]{2,1,0:T(8,128)}, u32[]{:S(2)}, u32[]{:S(2)}) collective-permute-start(f32[4,192,128]{2,1,0:T(8,128)S(1)} %get-tuple-element.32), channel_id=1, source_target_pairs={{0,4},{4,8},{8,12},{12,16},{16,20},{20,24},{24,28},{28,32},{32,36}... | collective-permute-start | bytes 1179656 | tf_op jit(solution)/shard_map/ppermute | solution.py:17
  175.5 16.2 %collective-permute-start.15 = (f32[4,192,128]{2,1,0:T(8,128)S(1)}, f32[4,192,128]{2,1,0:T(8,128)}, u32[]{:S(2)}, u32[]{:S(2)}) collective-permute-start(f32[4,192,128]{2,1,0:T(8,128)S(1)} %get-tuple-element.31), channel_id=1, source_target_pairs={{4,0},{8,4},{12,8},{16,12},{20,16},{24,20},{28,24},{32,28},{36,32}... | collective-permute-start | bytes 1179656 | tf_op jit(solution)/shard_map/ppermute | solution.py:18
  196.4 17.6 %collective-permute-start.16 = (f32[4,192,128]{2,1,0:T(8,128)S(1)}, f32[4,192,128]{2,1,0:T(8,128)S(1)}, u32[]{:S(2)}, u32[]{:S(2)}) collective-permute-start(f32[4,192,128]{2,1,0:T(8,128)S(1)} %get-tuple-element.30), channel_id=1, source_target_pairs={{0,4},{4,8},{8,12},{12,16},{16,20},{20,24},{24,28},{28,32},{32,36}... | collective-permute-start | bytes 1179656 | tf_op jit(solution)/shard_map/ppermute | solution.py:17
  199.4 16.7 %collective-permute-start.17 = (f32[4,192,128]{2,1,0:T(8,128)S(1)}, f32[4,192,128]{2,1,0:T(8,128)S(1)}, u32[]{:S(2)}, u32[]{:S(2)}) collective-permute-start(f32[4,192,128]{2,1,0:T(8,128)S(1)} %get-tuple-element.29), channel_id=1, source_target_pairs={{4,0},{8,4},{12,8},{16,12},{20,16},{24,20},{28,24},{32,28},{36,32}... | collective-permute-start | bytes 1179656 | tf_op jit(solution)/shard_map/ppermute | solution.py:18
  221.6 13.7 %copy-start.14 = (f32[8,192,128]{2,1,0:T(8,128)S(1)}, f32[8,192,128]{2,1,0:T(8,128)}, u32[]{:S(2)}) copy-start(f32[8,192,128]{2,1,0:T(8,128)} %shard_map.107.current.former) | copy-start | bytes 2359300
  221.6 17.6 %collective-permute-start.18 = (f32[4,192,128]{2,1,0:T(8,128)S(1)}, f32[4,192,128]{2,1,0:T(8,128)S(1)}, u32[]{:S(2)}, u32[]{:S(2)}) collective-permute-start(f32[4,192,128]{2,1,0:T(8,128)S(1)} %get-tuple-element.28), channel_id=1, source_target_pairs={{0,4},{4,8},{8,12},{12,16},{16,20},{20,24},{24,28},{28,32},{32,36}... | collective-permute-start | bytes 1179656 | tf_op jit(solution)/shard_map/ppermute | solution.py:17
  224.6 21.1 %collective-permute-start.19 = (f32[4,192,128]{2,1,0:T(8,128)S(1)}, f32[4,192,128]{2,1,0:T(8,128)S(1)}, u32[]{:S(2)}, u32[]{:S(2)}) collective-permute-start(f32[4,192,128]{2,1,0:T(8,128)S(1)} %get-tuple-element.27), channel_id=1, source_target_pairs={{4,0},{8,4},{12,8},{16,12},{20,16},{24,20},{28,24},{32,28},{36,32}... | collective-permute-start | bytes 1179656 | tf_op jit(solution)/shard_map/ppermute | solution.py:18
  251.1 13.4 %copy-start.16 = (f32[8,192,128]{2,1,0:T(8,128)S(1)}, f32[8,192,128]{2,1,0:T(8,128)}, u32[]{:S(2)}) copy-start(f32[8,192,128]{2,1,0:T(8,128)} %shard_map.108.current) | copy-start | bytes 2359300
  251.2 20.8 %collective-permute-start.20 = (f32[4,192,128]{2,1,0:T(8,128)S(1)}, f32[4,192,128]{2,1,0:T(8,128)S(1)}, u32[]{:S(2)}, u32[]{:S(2)}) collective-permute-start(f32[4,192,128]{2,1,0:T(8,128)S(1)} %get-tuple-element.26), channel_id=1, source_target_pairs={{0,4},{4,8},{8,12},{12,16},{16,20},{20,24},{24,28},{28,32},{32,36}... | collective-permute-start | bytes 1179656 | tf_op jit(solution)/shard_map/ppermute | solution.py:17
  254.1 17.9 %collective-permute-start.21 = (f32[4,192,128]{2,1,0:T(8,128)S(1)}, f32[4,192,128]{2,1,0:T(8,128)S(1)}, u32[]{:S(2)}, u32[]{:S(2)}) collective-permute-start(f32[4,192,128]{2,1,0:T(8,128)S(1)} %get-tuple-element.25), channel_id=1, source_target_pairs={{4,0},{8,4},{12,8},{16,12},{20,16},{24,20},{28,24},{32,28},{36,32}... | collective-permute-start | bytes 1179656 | tf_op jit(solution)/shard_map/ppermute | solution.py:18
  293.2 24.2 %collective-permute-start.22 = (f32[4,192,128]{2,1,0:T(8,128)S(1)}, f32[4,192,128]{2,1,0:T(8,128)S(1)}, u32[]{:S(2)}, u32[]{:S(2)}) collective-permute-start(f32[4,192,128]{2,1,0:T(8,128)S(1)} %get-tuple-element.24), channel_id=1, source_target_pairs={{0,4},{4,8},{8,12},{12,16},{16,20},{20,24},{24,28},{28,32},{32,36}... | collective-permute-start | bytes 1179656 | tf_op jit(solution)/shard_map/ppermute | solution.py:17
  295.9 21.4 %collective-permute-start.23 = (f32[4,192,128]{2,1,0:T(8,128)S(1)}, f32[4,192,128]{2,1,0:T(8,128)S(1)}, u32[]{:S(2)}, u32[]{:S(2)}) collective-permute-start(f32[4,192,128]{2,1,0:T(8,128)S(1)} %get-tuple-element.23), channel_id=1, source_target_pairs={{4,0},{8,4},{12,8},{16,12},{20,16},{24,20},{28,24},{32,28},{36,32}... | collective-permute-start | bytes 1179656 | tf_op jit(solution)/shard_map/ppermute | solution.py:18
  323.0 14.8 %copy-start.18 = (f32[8,192,128]{2,1,0:T(8,128)S(1)}, f32[8,192,128]{2,1,0:T(8,128)}, u32[]{:S(2)}) copy-start(f32[8,192,128]{2,1,0:T(8,128)} %shard_map.111.current.former) | copy-start | bytes 2359300
  323.0 18.1 %collective-permute-start.24 = (f32[4,192,128]{2,1,0:T(8,128)S(1)}, f32[4,192,128]{2,1,0:T(8,128)S(1)}, u32[]{:S(2)}, u32[]{:S(2)}) collective-permute-start(f32[4,192,128]{2,1,0:T(8,128)S(1)} %get-tuple-element.22), channel_id=1, source_target_pairs={{0,4},{4,8},{8,12},{12,16},{16,20},{20,24},{24,28},{28,32},{32,36}... | collective-permute-start | bytes 1179656 | tf_op jit(solution)/shard_map/ppermute | solution.py:17
  325.0 16.0 %collective-permute-start.25 = (f32[4,192,128]{2,1,0:T(8,128)S(1)}, f32[4,192,128]{2,1,0:T(8,128)S(1)}, u32[]{:S(2)}, u32[]{:S(2)}) collective-permute-start(f32[4,192,128]{2,1,0:T(8,128)S(1)} %get-tuple-element.21), channel_id=1, source_target_pairs={{4,0},{8,4},{12,8},{16,12},{20,16},{24,20},{28,24},{32,28},{36,32}... | collective-permute-start | bytes 1179656 | tf_op jit(solution)/shard_map/ppermute | solution.py:18
  346.7 24.2 %collective-permute-start.26 = (f32[4,192,128]{2,1,0:T(8,128)S(1)}, f32[4,192,128]{2,1,0:T(8,128)S(1)}, u32[]{:S(2)}, u32[]{:S(2)}) collective-permute-start(f32[4,192,128]{2,1,0:T(8,128)S(1)} %get-tuple-element.20), channel_id=1, source_target_pairs={{0,4},{4,8},{8,12},{12,16},{16,20},{20,24},{24,28},{28,32},{32,36}... | collective-permute-start | bytes 1179656 | tf_op jit(solution)/shard_map/ppermute | solution.py:17
  348.9 21.9 %collective-permute-start.27 = (f32[4,192,128]{2,1,0:T(8,128)S(1)}, f32[4,192,128]{2,1,0:T(8,128)S(1)}, u32[]{:S(2)}, u32[]{:S(2)}) collective-permute-start(f32[4,192,128]{2,1,0:T(8,128)S(1)} %get-tuple-element.19), channel_id=1, source_target_pairs={{4,0},{8,4},{12,8},{16,12},{20,16},{24,20},{28,24},{32,28},{36,32}... | collective-permute-start | bytes 1179656 | tf_op jit(solution)/shard_map/ppermute | solution.py:18
  376.4 15.1 %copy-start.20 = (f32[8,192,128]{2,1,0:T(8,128)S(1)}, f32[8,192,128]{2,1,0:T(8,128)}, u32[]{:S(2)}) copy-start(f32[8,192,128]{2,1,0:T(8,128)} %shard_map.113.current.former) | copy-start | bytes 2359300
  376.4 18.4 %collective-permute-start.28 = (f32[4,192,128]{2,1,0:T(8,128)S(1)}, f32[4,192,128]{2,1,0:T(8,128)S(1)}, u32[]{:S(2)}, u32[]{:S(2)}) collective-permute-start(f32[4,192,128]{2,1,0:T(8,128)S(1)} %get-tuple-element.18), channel_id=1, source_target_pairs={{0,4},{4,8},{8,12},{12,16},{16,20},{20,24},{24,28},{28,32},{32,36}... | collective-permute-start | bytes 1179656 | tf_op jit(solution)/shard_map/ppermute | solution.py:17
  378.5 16.4 %collective-permute-start.29 = (f32[4,192,128]{2,1,0:T(8,128)S(1)}, f32[4,192,128]{2,1,0:T(8,128)S(1)}, u32[]{:S(2)}, u32[]{:S(2)}) collective-permute-start(f32[4,192,128]{2,1,0:T(8,128)S(1)} %get-tuple-element.17), channel_id=1, source_target_pairs={{4,0},{8,4},{12,8},{16,12},{20,16},{24,20},{28,24},{32,28},{36,32}... | collective-permute-start | bytes 1179656 | tf_op jit(solution)/shard_map/ppermute | solution.py:18
  400.5 26.5 %collective-permute-start.30 = (f32[4,192,128]{2,1,0:T(8,128)S(1)}, f32[4,192,128]{2,1,0:T(8,128)S(1)}, u32[]{:S(2)}, u32[]{:S(2)}) collective-permute-start(f32[4,192,128]{2,1,0:T(8,128)S(1)} %get-tuple-element.16), channel_id=1, source_target_pairs={{0,4},{4,8},{8,12},{12,16},{16,20},{20,24},{24,28},{28,32},{32,36}... | collective-permute-start | bytes 1179656 | tf_op jit(solution)/shard_map/ppermute | solution.py:17
  402.7 24.3 %collective-permute-start.31 = (f32[4,192,128]{2,1,0:T(8,128)S(1)}, f32[4,192,128]{2,1,0:T(8,128)}, u32[]{:S(2)}, u32[]{:S(2)}) collective-permute-start(f32[4,192,128]{2,1,0:T(8,128)S(1)} %get-tuple-element.15), channel_id=1, source_target_pairs={{4,0},{8,4},{12,8},{16,12},{20,16},{24,20},{28,24},{32,28},{36,32}... | collective-permute-start | bytes 1179656 | tf_op jit(solution)/shard_map/ppermute | solution.py:18
  432.4 15.1 %copy-start.22 = (f32[8,192,128]{2,1,0:T(8,128)S(1)}, f32[8,192,128]{2,1,0:T(8,128)}, u32[]{:S(2)}) copy-start(f32[8,192,128]{2,1,0:T(8,128)} %shard_map.115.current.former) | copy-start | bytes 2359300
  432.4 18.4 %collective-permute-start.32 = (f32[4,192,128]{2,1,0:T(8,128)S(1)}, f32[4,192,128]{2,1,0:T(8,128)S(1)}, u32[]{:S(2)}, u32[]{:S(2)}) collective-permute-start(f32[4,192,128]{2,1,0:T(8,128)S(1)} %get-tuple-element.14), channel_id=1, source_target_pairs={{0,4},{4,8},{8,12},{12,16},{16,20},{20,24},{24,28},{28,32},{32,36}... | collective-permute-start | bytes 1179656 | tf_op jit(solution)/shard_map/ppermute | solution.py:17
  434.5 16.4 %collective-permute-start.33 = (f32[4,192,128]{2,1,0:T(8,128)S(1)}, f32[4,192,128]{2,1,0:T(8,128)}, u32[]{:S(2)}, u32[]{:S(2)}) collective-permute-start(f32[4,192,128]{2,1,0:T(8,128)S(1)} %get-tuple-element.13), channel_id=1, source_target_pairs={{4,0},{8,4},{12,8},{16,12},{20,16},{24,20},{28,24},{32,28},{36,32}... | collective-permute-start | bytes 1179656 | tf_op jit(solution)/shard_map/ppermute | solution.py:18
  457.1 33.8 %collective-permute-start.34 = (f32[4,192,128]{2,1,0:T(8,128)}, f32[4,192,128]{2,1,0:T(8,128)}, u32[]{:S(2)}, u32[]{:S(2)}) collective-permute-start(f32[4,192,128]{2,1,0:T(8,128)} %get-tuple-element.12), channel_id=1, source_target_pairs={{0,4},{4,8},{8,12},{12,16},{16,20},{20,24},{24,28},{28,32},{32,36}... | collective-permute-start | bytes 1179656 | tf_op jit(solution)/shard_map/ppermute | solution.py:17
  459.0 31.8 %collective-permute-start.35 = (f32[4,192,128]{2,1,0:T(8,128)S(1)}, f32[4,192,128]{2,1,0:T(8,128)}, u32[]{:S(2)}, u32[]{:S(2)}) collective-permute-start(f32[4,192,128]{2,1,0:T(8,128)S(1)} %get-tuple-element.11), channel_id=1, source_target_pairs={{4,0},{8,4},{12,8},{16,12},{20,16},{24,20},{28,24},{32,28},{36,32}... | collective-permute-start | bytes 1179656 | tf_op jit(solution)/shard_map/ppermute | solution.py:18
  496.3 26.7 %collective-permute-start.36 = (f32[4,192,128]{2,1,0:T(8,128)}, f32[4,192,128]{2,1,0:T(8,128)}, u32[]{:S(2)}, u32[]{:S(2)}) collective-permute-start(f32[4,192,128]{2,1,0:T(8,128)} %get-tuple-element.10), channel_id=1, source_target_pairs={{0,4},{4,8},{8,12},{12,16},{16,20},{20,24},{24,28},{28,32},{32,36}... | collective-permute-start | bytes 1179656 | tf_op jit(solution)/shard_map/ppermute | solution.py:17
  498.2 24.8 %collective-permute-start.37 = (f32[4,192,128]{2,1,0:T(8,128)S(1)}, f32[4,192,128]{2,1,0:T(8,128)}, u32[]{:S(2)}, u32[]{:S(2)}) collective-permute-start(f32[4,192,128]{2,1,0:T(8,128)S(1)} %get-tuple-element.9), channel_id=1, source_target_pairs={{4,0},{8,4},{12,8},{16,12},{20,16},{24,20},{28,24},{32,28},{36,32}... | collective-permute-start | bytes 1179656 | tf_op jit(solution)/shard_map/ppermute | solution.py:18
  528.5 25.8 %collective-permute-start.38 = (f32[4,192,128]{2,1,0:T(8,128)}, f32[4,192,128]{2,1,0:T(8,128)}, u32[]{:S(2)}, u32[]{:S(2)}) collective-permute-start(f32[4,192,128]{2,1,0:T(8,128)} %get-tuple-element.8), channel_id=1, source_target_pairs={{0,4},{4,8},{8,12},{12,16},{16,20},{20,24},{24,28},{28,32},{32,36}... | collective-permute-start | bytes 1179656 | tf_op jit(solution)/shard_map/ppermute | solution.py:17
  530.4 23.9 %collective-permute-start.39 = (f32[4,192,128]{2,1,0:T(8,128)S(1)}, f32[4,192,128]{2,1,0:T(8,128)}, u32[]{:S(2)}, u32[]{:S(2)}) collective-permute-start(f32[4,192,128]{2,1,0:T(8,128)S(1)} %get-tuple-element.7), channel_id=1, source_target_pairs={{4,0},{8,4},{12,8},{16,12},{20,16},{24,20},{28,24},{32,28},{36,32}... | collective-permute-start | bytes 1179656 | tf_op jit(solution)/shard_map/ppermute | solution.py:18
  565.8 3.6 collective-permute-start.40
  570.4 10.3 %collective-permute-start.41 = (f32[8,48,128]{2,1,0:T(8,128)S(1)}, f32[8,48,128]{2,1,0:T(8,128)S(1)}, u32[]{:S(2)}, u32[]{:S(2)}) collective-permute-start(f32[8,48,128]{2,1,0:T(8,128)S(1)} %dynamic-slice_bitcast_fusion.1), channel_id=1, source_target_pairs={{0,2},{1,3},{2,0},{3,1},{4,6},{5,7},{6,4},{7,5},{8,10},{9,11},{10,... | collective-permute-start | bytes 589832 | tf_op jit(solution)/shard_map/ppermute | solution.py:153
  (65 other events, 389.6 us)

commit v3 on v2

--- a/solution.py
+++ b/solution.py
@@ -87,10 +87,11 @@
     )(current, former, courant_sq, interior, low, high, injected)
 
 
-def step(current, former, courant_sq, injected):
+def step(current, former, courant_sq, injected, held=None):
     low, high = exchange_edges(current)
-    interior = inner_laplace(current)
-    return fused_update(current, former, courant_sq, interior, low, high, injected)
+    interior, held = lax.optimization_barrier((inner_laplace(current), held))
+    lap = interior + edge_terms(low, high, current.shape[0])
+    return 2.0 * current - former + courant_sq * lap + injected, held
 
 
 def per_device(
@@ -121,7 +122,7 @@
     traces = []
     for t in range(steps):
         injected = empty_flat.at[source_index].add(jnp.where(inside, pulses[t], 0.0))
-        latest = step(current, former, courant_sq, injected.reshape(velocity.shape))
+        latest, _ = step(current, former, courant_sq, injected.reshape(velocity.shape))
         accelerations.append(latest - 2.0 * current + former)
         traces.append(latest.reshape(-1)[receiver_cells])
         current, former = latest, current
@@ -133,11 +134,17 @@
 
     following, furthest = adjoint_now[0], adjoint_prev[0]
     imaging = jnp.zeros_like(velocity)
+    pending = None
     for t in reversed(range(steps)):
         injected = empty_flat.at[receiver_cells].add(misfit[t])
-        earlier = step(following, furthest, courant_sq, injected.reshape(velocity.shape))
-        imaging = imaging + earlier * accelerations[t]
+        earlier, pending = step(
+            following, furthest, courant_sq, injected.reshape(velocity.shape), pending
+        )
+        if pending is not None:
+            imaging = imaging + pending * accelerations[t + 1]
+        pending = earlier
         following, furthest = earlier, following
+    imaging = imaging + pending * accelerations[0]
 
     shots = lax.axis_size("shot")
     shot = lax.axis_index("shot")

time: 594 us -> 650 us (1.094)
  the two profiles are of different devices: /device:TPU:388 before, /device:TPU:382 now
where the time goes in v3:
time: 650 us; the launch traced here: 638 us
  other arithmetic  312 us (48%)
  starting transfers between devices  207 us (32%)
  local copies, waits for them, and re-layouts  83.4 us (13%)
  waiting for transfers between devices  33.5 us (5%)
    add x20, other arithmetic, inner_laplace(): result = result + TAPS[distance] * beside_all  184 us
    ppermute x20, starting transfers between devices, exchange_edges(): low = lax.ppermute(block[block.shape[0] - RADIUS:], 'space', forward)  159 us
    gather x10, local copies, waits for them, and re-layouts, per_device(): traces.append(latest.reshape(-1)[receiver_cells])  63.6 us
    add x19, other arithmetic, step(): return (2.0 * current - former + courant_sq * lap + injected, held)  45.3 us
    scatter-add x10, other arithmetic, per_device(): injected = empty_flat.at[receiver_cells].add(misfit[t])  44.2 us
    ppermute x20, starting transfers between devices, exchange_edges(): high = lax.ppermute(block[:RADIUS], 'space', backward)  42.4 us
    scatter-add x10, other arithmetic, per_device(): empty_flat.at[source_index].add(jnp.where(inside, pulses[t], 0.0))  25 us
    slice x20, local copies, waits for them, and re-layouts, exchange_edges(): low = lax.ppermute(block[block.shape[0] - RADIUS:], 'space', forward)  16.9 us
  transfers between devices with their start and end apart: 42, of which 9 were waited for; matrix products, arithmetic and copies ran while one was open for 53% of the time, Pallas kernels for 0%

profile of v3, /device:TPU:382, one launch (start us, length us, event | category | flops | bytes accessed | tf_op | source)
XLA Modules:
  0.0 638.0 jit_solution(3202413777174536004)
XLA Ops:
  4.0 7.3 %collective-permute-start.3 = (f32[4,192,128]{2,1,0:T(8,128)S(1)}, f32[4,192,128]{2,1,0:T(8,128)}, u32[]{:S(2)}, u32[]{:S(2)}) collective-permute-start(f32[4,192,128]{2,1,0:T(8,128)S(1)} %get-tuple-element.83), channel_id=1, source_target_pairs={{0,4},{4,8},{8,12},{12,16},{16,20},{20,24},{24,28},{28,32},{32,36}... | collective-permute-start | bytes 1179656 | tf_op jit(solution)/shard_map/ppermute | solution.py:17
  27.6 7.3 %collective-permute-start.5 = (f32[4,192,128]{2,1,0:T(8,128)S(1)}, f32[4,192,128]{2,1,0:T(8,128)}, u32[]{:S(2)}, u32[]{:S(2)}) collective-permute-start(f32[4,192,128]{2,1,0:T(8,128)S(1)} %get-tuple-element.81), channel_id=1, source_target_pairs={{0,4},{4,8},{8,12},{12,16},{16,20},{20,24},{24,28},{28,32},{32,36}... | collective-permute-start | bytes 1179656 | tf_op jit(solution)/shard_map/ppermute | solution.py:17
  49.7 7.3 %collective-permute-start.7 = (f32[4,192,128]{2,1,0:T(8,128)S(1)}, f32[4,192,128]{2,1,0:T(8,128)}, u32[]{:S(2)}, u32[]{:S(2)}) collective-permute-start(f32[4,192,128]{2,1,0:T(8,128)S(1)} %get-tuple-element.79), channel_id=1, source_target_pairs={{0,4},{4,8},{8,12},{12,16},{16,20},{20,24},{24,28},{28,32},{32,36}... | collective-permute-start | bytes 1179656 | tf_op jit(solution)/shard_map/ppermute | solution.py:17
  71.7 7.3 %collective-permute-start.9 = (f32[4,192,128]{2,1,0:T(8,128)S(1)}, f32[4,192,128]{2,1,0:T(8,128)}, u32[]{:S(2)}, u32[]{:S(2)}) collective-permute-start(f32[4,192,128]{2,1,0:T(8,128)S(1)} %get-tuple-element.77), channel_id=1, source_target_pairs={{0,4},{4,8},{8,12},{12,16},{16,20},{20,24},{24,28},{28,32},{32,36}... | collective-permute-start | bytes 1179656 | tf_op jit(solution)/shard_map/ppermute | solution.py:17
  84.1 11.5 %collective-permute-done.9 = f32[4,192,128]{2,1,0:T(8,128)} collective-permute-done((f32[4,192,128]{2,1,0:T(8,128)S(1)}, f32[4,192,128]{2,1,0:T(8,128)}, u32[]{:S(2)}, u32[]{:S(2)}) %collective-permute-start.9) | collective-permute-done | bytes 393248 | tf_op jit(solution)/shard_map/ppermute | solution.py:17
  101.6 7.7 %collective-permute-start.11 = (f32[4,192,128]{2,1,0:T(8,128)S(1)}, f32[4,192,128]{2,1,0:T(8,128)}, u32[]{:S(2)}, u32[]{:S(2)}) collective-permute-start(f32[4,192,128]{2,1,0:T(8,128)S(1)} %get-tuple-element.75), channel_id=1, source_target_pairs={{0,4},{4,8},{8,12},{12,16},{16,20},{20,24},{24,28},{28,32},{32,36}... | collective-permute-start | bytes 1179656 | tf_op jit(solution)/shard_map/ppermute | solution.py:17
  111.8 12.2 %fusion.451 = f32[8,192,128]{2,1,0:T(8,128)S(1)} fusion(f32[8,192,128]{2,1,0:T(8,128)} %copy-done.1), kind=kLoop, calls=%fused_computation.1121 | loop fusion | flops 5701632 | bytes 1572864 | tf_op jit(solution)/shard_map/add | solution.py:41
  129.2 8.1 %collective-permute-start.13 = (f32[4,192,128]{2,1,0:T(8,128)}, f32[4,192,128]{2,1,0:T(8,128)}, u32[]{:S(2)}, u32[]{:S(2)}) collective-permute-start(f32[4,192,128]{2,1,0:T(8,128)} %get-tuple-element.73), channel_id=1, source_target_pairs={{0,4},{4,8},{8,12},{12,16},{16,20},{20,24},{24,28},{28,32},{32,36}... | collective-permute-start | bytes 1179656 | tf_op jit(solution)/shard_map/ppermute | solution.py:17
  140.1 8.1 %collective-permute-start.1 = (f32[4,192,128]{2,1,0:T(8,128)S(1)}, f32[4,192,128]{2,1,0:T(8,128)}, u32[]{:S(2)}, u32[]{:S(2)}) collective-permute-start(f32[4,192,128]{2,1,0:T(8,128)S(1)} %get-tuple-element.63), channel_id=1, source_target_pairs={{0,4},{4,8},{8,12},{12,16},{16,20},{20,24},{24,28},{28,32},{32,36}... | collective-permute-start | bytes 1179656 | tf_op jit(solution)/shard_map/ppermute | solution.py:17
  150.7 10.9 %fusion.479 = f32[8,192,128]{2,1,0:T(8,128)S(1)} fusion(f32[8,192,128]{2,1,0:T(8,128)} %copy-done.5), kind=kLoop, calls=%fused_computation.1149 | loop fusion | flops 5701632 | bytes 1572864 | tf_op jit(solution)/shard_map/add | solution.py:41
  166.9 8.1 %collective-permute-start.15 = (f32[4,192,128]{2,1,0:T(8,128)}, f32[4,192,128]{2,1,0:T(8,128)}, u32[]{:S(2)}, u32[]{:S(2)}) collective-permute-start(f32[4,192,128]{2,1,0:T(8,128)} %get-tuple-element.71), channel_id=1, source_target_pairs={{0,4},{4,8},{8,12},{12,16},{16,20},{20,24},{24,28},{28,32},{32,36}... | collective-permute-start | bytes 1179656 | tf_op jit(solution)/shard_map/ppermute | solution.py:17
  180.8 10.9 %fusion.507 = f32[8,192,128]{2,1,0:T(8,128)S(1)} fusion(f32[8,192,128]{2,1,0:T(8,128)} %copy-done.9), kind=kLoop, calls=%fused_computation.1177 | loop fusion | flops 5701632 | bytes 1572864 | tf_op jit(solution)/shard_map/add | solution.py:41
  197.1 8.3 %collective-permute-start.17 = (f32[4,192,128]{2,1,0:T(8,128)}, f32[4,192,128]{2,1,0:T(8,128)}, u32[]{:S(2)}, u32[]{:S(2)}) collective-permute-start(f32[4,192,128]{2,1,0:T(8,128)} %get-tuple-element.69), channel_id=1, source_target_pairs={{0,4},{4,8},{8,12},{12,16},{16,20},{20,24},{24,28},{28,32},{32,36}... | collective-permute-start | bytes 1179656 | tf_op jit(solution)/shard_map/ppermute | solution.py:17
  208.5 10.8 %fusion.535 = f32[8,192,128]{2,1,0:T(8,128)S(1)} fusion(f32[8,192,128]{2,1,0:T(8,128)} %copy-done.12), kind=kLoop, calls=%fused_computation.1205 | loop fusion | flops 5701632 | bytes 1572864 | tf_op jit(solution)/shard_map/add | solution.py:41
  224.8 8.1 %collective-permute-start.19 = (f32[4,192,128]{2,1,0:T(8,128)}, f32[4,192,128]{2,1,0:T(8,128)}, u32[]{:S(2)}, u32[]{:S(2)}) collective-permute-start(f32[4,192,128]{2,1,0:T(8,128)} %get-tuple-element.67), channel_id=1, source_target_pairs={{0,4},{4,8},{8,12},{12,16},{16,20},{20,24},{24,28},{28,32},{32,36}... | collective-permute-start | bytes 1179656 | tf_op jit(solution)/shard_map/ppermute | solution.py:17
  236.0 10.7 %fusion.563 = f32[8,192,128]{2,1,0:T(8,128)S(1)} fusion(f32[8,192,128]{2,1,0:T(8,128)} %copy-done.15), kind=kLoop, calls=%fused_computation.1233 | loop fusion | flops 5701632 | bytes 1572864 | tf_op jit(solution)/shard_map/add | solution.py:41
  252.3 8.1 %collective-permute-start.21 = (f32[4,192,128]{2,1,0:T(8,128)}, f32[4,192,128]{2,1,0:T(8,128)}, u32[]{:S(2)}, u32[]{:S(2)}) collective-permute-start(f32[4,192,128]{2,1,0:T(8,128)} %get-tuple-element.65), channel_id=1, source_target_pairs={{0,4},{4,8},{8,12},{12,16},{16,20},{20,24},{24,28},{28,32},{32,36}... | collective-permute-start | bytes 1179656 | tf_op jit(solution)/shard_map/ppermute | solution.py:17
  263.6 11.9 %fusion.591 = f32[8,192,128]{2,1,0:T(8,128)} fusion(f32[8,192,128]{2,1,0:T(8,128)} %copy-done.17), kind=kLoop, calls=%fused_computation.1261 | loop fusion | flops 5701632 | bytes 1572864 | tf_op jit(solution)/shard_map/add | solution.py:41
  275.5 7.5 %gather_fusion.1 = f32[512]{0:T(512)} fusion(f32[196608]{0:T(1024)} %bitcast.127, s32[1024]{0:T(1024)S(1)} %pad_clamp_fusion), kind=kCustom, calls=%fused_computation.1 | custom fusion | bytes 6144 | tf_op jit(solution)/shard_map/gather | solution.py:127
  286.9 7.4 %gather_fusion = f32[512]{0:T(512)} fusion(f32[196608]{0:T(1024)} %bitcast.129, s32[1024]{0:T(1024)S(1)} %pad_clamp_fusion), kind=kCustom, calls=%fused_computation | custom fusion | bytes 6144 | tf_op jit(solution)/shard_map/gather | solution.py:127
  295.6 4.5 scatter_custom_fusion.10
  306.0 8.1 %collective-permute-start.23 = (f32[4,192,128]{2,1,0:T(8,128)S(1)}, f32[4,192,128]{2,1,0:T(8,128)}, u32[]{:S(2)}, u32[]{:S(2)}) collective-permute-start(f32[4,192,128]{2,1,0:T(8,128)S(1)} %get-tuple-element.61), channel_id=1, source_target_pairs={{0,4},{4,8},{8,12},{12,16},{16,20},{20,24},{24,28},{28,32},{32,36}... | collective-permute-start | bytes 1179656 | tf_op jit(solution)/shard_map/ppermute | solution.py:17
  314.2 7.4 %gather_fusion.3 = f32[512]{0:T(512)} fusion(f32[196608]{0:T(1024)} %bitcast.125, s32[1024]{0:T(1024)S(1)} %pad_clamp_fusion), kind=kCustom, calls=%fused_computation.3 | custom fusion | bytes 6144 | tf_op jit(solution)/shard_map/gather | solution.py:127
  321.6 7.4 %gather_fusion.2 = f32[512]{0:T(512)} fusion(f32[196608]{0:T(1024)} %bitcast.126, s32[1024]{0:T(1024)S(1)} %pad_clamp_fusion), kind=kCustom, calls=%fused_computation.2 | custom fusion | bytes 6144 | tf_op jit(solution)/shard_map/gather | solution.py:127
  329.0 11.9 %fusion.619 = f32[8,192,128]{2,1,0:T(8,128)} fusion(f32[8,192,128]{2,1,0:T(8,128)} %copy-done.18), kind=kLoop, calls=%fused_computation.1289 | loop fusion | flops 5701632 | bytes 1572864 | tf_op jit(solution)/shard_map/add | solution.py:41
  351.1 8.1 %collective-permute-start.25 = (f32[4,192,128]{2,1,0:T(8,128)S(1)}, f32[4,192,128]{2,1,0:T(8,128)}, u32[]{:S(2)}, u32[]{:S(2)}) collective-permute-start(f32[4,192,128]{2,1,0:T(8,128)S(1)} %get-tuple-element.59), channel_id=1, source_target_pairs={{0,4},{4,8},{8,12},{12,16},{16,20},{20,24},{24,28},{28,32},{32,36}... | collective-permute-start | bytes 1179656 | tf_op jit(solution)/shard_map/ppermute | solution.py:17
  364.2 11.4 %fusion.647 = f32[8,192,128]{2,1,0:T(8,128)S(1)} fusion(f32[8,192,128]{2,1,0:T(8,128)} %copy-done.20), kind=kLoop, calls=%fused_computation.1317 | loop fusion | flops 5701632 | bytes 1572864 | tf_op jit(solution)/shard_map/add | solution.py:41
  381.1 8.1 %collective-permute-start.27 = (f32[4,192,128]{2,1,0:T(8,128)S(1)}, f32[4,192,128]{2,1,0:T(8,128)}, u32[]{:S(2)}, u32[]{:S(2)}) collective-permute-start(f32[4,192,128]{2,1,0:T(8,128)S(1)} %get-tuple-element.57), channel_id=1, source_target_pairs={{0,4},{4,8},{8,12},{12,16},{16,20},{20,24},{24,28},{28,32},{32,36}... | collective-permute-start | bytes 1179656 | tf_op jit(solution)/shard_map/ppermute | solution.py:17
  389.2 7.4 %gather_fusion.5 = f32[512]{0:T(512)} fusion(f32[196608]{0:T(1024)} %bitcast.123, s32[1024]{0:T(1024)S(1)} %pad_clamp_fusion), kind=kCustom, calls=%fused_computation.5 | custom fusion | bytes 6144 | tf_op jit(solution)/shard_map/gather | solution.py:127
  396.6 7.4 %gather_fusion.4 = f32[512]{0:T(512)} fusion(f32[196608]{0:T(1024)} %bitcast.124, s32[1024]{0:T(1024)S(1)} %pad_clamp_fusion), kind=kCustom, calls=%fused_computation.4 | custom fusion | bytes 6144 | tf_op jit(solution)/shard_map/gather | solution.py:127
  404.1 4.8 scatter_custom_fusion.13
  408.8 11.3 %fusion.675 = f32[8,192,128]{2,1,0:T(8,128)S(1)} fusion(f32[8,192,128]{2,1,0:T(8,128)} %copy-done.23), kind=kLoop, calls=%fused_computation.1345 | loop fusion | flops 5701632 | bytes 1572864 | tf_op jit(solution)/shard_map/add | solution.py:41
  425.5 8.1 %collective-permute-start.29 = (f32[4,192,128]{2,1,0:T(8,128)S(1)}, f32[4,192,128]{2,1,0:T(8,128)}, u32[]{:S(2)}, u32[]{:S(2)}) collective-permute-start(f32[4,192,128]{2,1,0:T(8,128)S(1)} %get-tuple-element.55), channel_id=1, source_target_pairs={{0,4},{4,8},{8,12},{12,16},{16,20},{20,24},{24,28},{28,32},{32,36}... | collective-permute-start | bytes 1179656 | tf_op jit(solution)/shard_map/ppermute | solution.py:17
  438.7 12.1 %fusion.703 = f32[8,192,128]{2,1,0:T(8,128)S(1)} fusion(f32[8,192,128]{2,1,0:T(8,128)} %copy-done.26), kind=kLoop, calls=%fused_computation.1373 | loop fusion | flops 5701632 | bytes 1572864 | tf_op jit(solution)/shard_map/add | solution.py:41
  456.1 8.1 %collective-permute-start.31 = (f32[4,192,128]{2,1,0:T(8,128)S(1)}, f32[4,192,128]{2,1,0:T(8,128)}, u32[]{:S(2)}, u32[]{:S(2)}) collective-permute-start(f32[4,192,128]{2,1,0:T(8,128)S(1)} %get-tuple-element.53), channel_id=1, source_target_pairs={{0,4},{4,8},{8,12},{12,16},{16,20},{20,24},{24,28},{28,32},{32,36}... | collective-permute-start | bytes 1179656 | tf_op jit(solution)/shard_map/ppermute | solution.py:17
  468.5 7.5 %gather_fusion.6 = f32[512]{0:T(512)} fusion(f32[196608]{0:T(1024)} %bitcast.122, s32[1024]{0:T(1024)S(1)} %pad_clamp_fusion), kind=kCustom, calls=%fused_computation.6 | custom fusion | bytes 6144 | tf_op jit(solution)/shard_map/gather | solution.py:127
  480.4 11.2 %fusion.731 = f32[8,192,128]{2,1,0:T(8,128)S(1)} fusion(f32[8,192,128]{2,1,0:T(8,128)} %copy-done.29), kind=kLoop, calls=%fused_computation.1401 | loop fusion | flops 5701632 | bytes 1572864 | tf_op jit(solution)/shard_map/add | solution.py:41
  496.8 8.3 %collective-permute-start.33 = (f32[4,192,128]{2,1,0:T(8,128)S(1)}, f32[4,192,128]{2,1,0:T(8,128)}, u32[]{:S(2)}, u32[]{:S(2)}) collective-permute-start(f32[4,192,128]{2,1,0:T(8,128)S(1)} %get-tuple-element.51), channel_id=1, source_target_pairs={{0,4},{4,8},{8,12},{12,16},{16,20},{20,24},{24,28},{28,32},{32,36}... | collective-permute-start | bytes 1179656 | tf_op jit(solution)/shard_map/ppermute | solution.py:17
  510.1 11.0 %fusion.759 = f32[8,192,128]{2,1,0:T(8,128)S(1)} fusion(f32[8,192,128]{2,1,0:T(8,128)} %copy-done.32), kind=kLoop, calls=%fused_computation.1429 | loop fusion | flops 5701632 | bytes 1572864 | tf_op jit(solution)/shard_map/add | solution.py:41
  526.4 8.1 %collective-permute-start.35 = (f32[4,192,128]{2,1,0:T(8,128)S(1)}, f32[4,192,128]{2,1,0:T(8,128)}, u32[]{:S(2)}, u32[]{:S(2)}) collective-permute-start(f32[4,192,128]{2,1,0:T(8,128)S(1)} %get-tuple-element.49), channel_id=1, source_target_pairs={{0,4},{4,8},{8,12},{12,16},{16,20},{20,24},{24,28},{28,32},{32,36}... | collective-permute-start | bytes 1179656 | tf_op jit(solution)/shard_map/ppermute | solution.py:17
  546.3 10.5 %fusion.787 = f32[8,192,128]{2,1,0:T(8,128)S(1)} fusion(f32[8,192,128]{2,1,0:T(8,128)} %copy-done.35), kind=kLoop, calls=%fused_computation.1457 | loop fusion | flops 5701632 | bytes 1572864 | tf_op jit(solution)/shard_map/add | solution.py:41
  562.2 8.1 %collective-permute-start.37 = (f32[4,192,128]{2,1,0:T(8,128)S(1)}, f32[4,192,128]{2,1,0:T(8,128)}, u32[]{:S(2)}, u32[]{:S(2)}) collective-permute-start(f32[4,192,128]{2,1,0:T(8,128)S(1)} %get-tuple-element.47), channel_id=1, source_target_pairs={{0,4},{4,8},{8,12},{12,16},{16,20},{20,24},{24,28},{28,32},{32,36}... | collective-permute-start | bytes 1179656 | tf_op jit(solution)/shard_map/ppermute | solution.py:17
  571.0 4.5 scatter_custom_fusion.18
  575.6 10.8 %fusion.815 = f32[8,192,128]{2,1,0:T(8,128)S(1)} fusion(f32[8,192,128]{2,1,0:T(8,128)} %copy-done.39), kind=kLoop, calls=%fused_computation.1485 | loop fusion | flops 5701632 | bytes 1572864 | tf_op jit(solution)/shard_map/add | solution.py:41
  591.8 8.1 %collective-permute-start.39 = (f32[4,192,128]{2,1,0:T(8,128)S(1)}, f32[4,192,128]{2,1,0:T(8,128)}, u32[]{:S(2)}, u32[]{:S(2)}) collective-permute-start(f32[4,192,128]{2,1,0:T(8,128)S(1)} %get-tuple-element.45), channel_id=1, source_target_pairs={{0,4},{4,8},{8,12},{12,16},{16,20},{20,24},{24,28},{28,32},{32,36}... | collective-permute-start | bytes 1179656 | tf_op jit(solution)/shard_map/ppermute | solution.py:17
  604.4 11.8 %fusion.843 = f32[8,192,128]{2,1,0:T(8,128)S(1)} fusion(f32[8,192,128]{2,1,0:T(8,128)} %copy-done.41), kind=kLoop, calls=%fused_computation.1513 | loop fusion | flops 5701632 | bytes 1572864 | tf_op jit(solution)/shard_map/add | solution.py:41
  616.2 6.7 %fusion.295 = f32[8,192,128]{2,1,0:T(8,128)S(1)} fusion(f32[8,192,128]{2,1,0:T(8,128)} %bitcast.131, f32[8,192,128]{2,1,0:T(8,128)S(1)} %fusion.843, f32[4,192,128]{2,1,0:T(8,128)} %collective-permute-done.38, f32[4,192,128]{2,1,0:T(8,128)} %collective-permute-done.39, f32[1,8,192,128]{3,2,1,0:T(8,128)} %param.12, f32[8,192,128]{2,1,0:T(8,128)S(1)} %fusion.23, ...), kind=kLoop, calls=%fused_computation.965 | loop fusion | flops 13369344 | bytes 20447232 | tf_op jit(solution)/shard_map/add | solution.py:147
  630.1 7.0 %collective-permute-done.41 = f32[8,48,128]{2,1,0:T(8,128)S(1)} collective-permute-done((f32[8,48,128]{2,1,0:T(8,128)S(1)}, f32[8,48,128]{2,1,0:T(8,128)S(1)}, u32[]{:S(2)}, u32[]{:S(2)}) %collective-permute-start.41) | collective-permute-done | bytes 196640 | tf_op jit(solution)/shard_map/ppermute | solution.py:160
  (274 shorter events, 215.7 us)
Async XLA Ops:
  1.2 19.5 %collective-permute-start.2 = (f32[4,192,128]{2,1,0:T(8,128)S(1)}, f32[4,192,128]{2,1,0:T(8,128)S(1)}, u32[]{:S(2)}, u32[]{:S(2)}) collective-permute-start(f32[4,192,128]{2,1,0:T(8,128)S(1)} %get-tuple-element.84), channel_id=1, source_target_pairs={{4,0},{8,4},{12,8},{16,12},{20,16},{24,20},{28,24},{32,28},{36,32}... | collective-permute-start | bytes 1179656 | tf_op jit(solution)/shard_map/ppermute | solution.py:18
  4.0 18.7 %collective-permute-start.3 = (f32[4,192,128]{2,1,0:T(8,128)S(1)}, f32[4,192,128]{2,1,0:T(8,128)}, u32[]{:S(2)}, u32[]{:S(2)}) collective-permute-start(f32[4,192,128]{2,1,0:T(8,128)S(1)} %get-tuple-element.83), channel_id=1, source_target_pairs={{0,4},{4,8},{8,12},{12,16},{16,20},{20,24},{24,28},{28,32},{32,36}... | collective-permute-start | bytes 1179656 | tf_op jit(solution)/shard_map/ppermute | solution.py:17
  24.8 18.7 %collective-permute-start.4 = (f32[4,192,128]{2,1,0:T(8,128)S(1)}, f32[4,192,128]{2,1,0:T(8,128)S(1)}, u32[]{:S(2)}, u32[]{:S(2)}) collective-permute-start(f32[4,192,128]{2,1,0:T(8,128)S(1)} %get-tuple-element.82), channel_id=1, source_target_pairs={{4,0},{8,4},{12,8},{16,12},{20,16},{24,20},{28,24},{32,28},{36,32}... | collective-permute-start | bytes 1179656 | tf_op jit(solution)/shard_map/ppermute | solution.py:18
  27.6 17.5 %collective-permute-start.5 = (f32[4,192,128]{2,1,0:T(8,128)S(1)}, f32[4,192,128]{2,1,0:T(8,128)}, u32[]{:S(2)}, u32[]{:S(2)}) collective-permute-start(f32[4,192,128]{2,1,0:T(8,128)S(1)} %get-tuple-element.81), channel_id=1, source_target_pairs={{0,4},{4,8},{8,12},{12,16},{16,20},{20,24},{24,28},{28,32},{32,36}... | collective-permute-start | bytes 1179656 | tf_op jit(solution)/shard_map/ppermute | solution.py:17
  46.9 17.8 %collective-permute-start.6 = (f32[4,192,128]{2,1,0:T(8,128)S(1)}, f32[4,192,128]{2,1,0:T(8,128)S(1)}, u32[]{:S(2)}, u32[]{:S(2)}) collective-permute-start(f32[4,192,128]{2,1,0:T(8,128)S(1)} %get-tuple-element.80), channel_id=1, source_target_pairs={{4,0},{8,4},{12,8},{16,12},{20,16},{24,20},{28,24},{32,28},{36,32}... | collective-permute-start | bytes 1179656 | tf_op jit(solution)/shard_map/ppermute | solution.py:18
  49.7 16.6 %collective-permute-start.7 = (f32[4,192,128]{2,1,0:T(8,128)S(1)}, f32[4,192,128]{2,1,0:T(8,128)}, u32[]{:S(2)}, u32[]{:S(2)}) collective-permute-start(f32[4,192,128]{2,1,0:T(8,128)S(1)} %get-tuple-element.79), channel_id=1, source_target_pairs={{0,4},{4,8},{8,12},{12,16},{16,20},{20,24},{24,28},{28,32},{32,36}... | collective-permute-start | bytes 1179656 | tf_op jit(solution)/shard_map/ppermute | solution.py:17
  68.9 15.2 %collective-permute-start.8 = (f32[4,192,128]{2,1,0:T(8,128)}, f32[4,192,128]{2,1,0:T(8,128)}, u32[]{:S(2)}, u32[]{:S(2)}) collective-permute-start(f32[4,192,128]{2,1,0:T(8,128)} %get-tuple-element.78), channel_id=1, source_target_pairs={{4,0},{8,4},{12,8},{16,12},{20,16},{24,20},{28,24},{32,28},{36,32}... | collective-permute-start | bytes 1179656 | tf_op jit(solution)/shard_map/ppermute | solution.py:18
  71.7 23.9 %collective-permute-start.9 = (f32[4,192,128]{2,1,0:T(8,128)S(1)}, f32[4,192,128]{2,1,0:T(8,128)}, u32[]{:S(2)}, u32[]{:S(2)}) collective-permute-start(f32[4,192,128]{2,1,0:T(8,128)S(1)} %get-tuple-element.77), channel_id=1, source_target_pairs={{0,4},{4,8},{8,12},{12,16},{16,20},{20,24},{24,28},{28,32},{32,36}... | collective-permute-start | bytes 1179656 | tf_op jit(solution)/shard_map/ppermute | solution.py:17
  81.5 14.0 %copy-start.47 = (f32[196608]{0:T(1024)S(1)}, f32[196608]{0:T(1024)}, u32[]{:S(2)}) copy-start(f32[196608]{0:T(1024)} %scatter_custom_fusion.3) | copy-start | bytes 2359300
  98.7 25.2 %collective-permute-start.10 = (f32[4,192,128]{2,1,0:T(8,128)}, f32[4,192,128]{2,1,0:T(8,128)}, u32[]{:S(2)}, u32[]{:S(2)}) collective-permute-start(f32[4,192,128]{2,1,0:T(8,128)} %get-tuple-element.76), channel_id=1, source_target_pairs={{4,0},{8,4},{12,8},{16,12},{20,16},{24,20},{28,24},{32,28},{36,32}... | collective-permute-start | bytes 1179656 | tf_op jit(solution)/shard_map/ppermute | solution.py:18
  101.6 22.4 %collective-permute-start.11 = (f32[4,192,128]{2,1,0:T(8,128)S(1)}, f32[4,192,128]{2,1,0:T(8,128)}, u32[]{:S(2)}, u32[]{:S(2)}) collective-permute-start(f32[4,192,128]{2,1,0:T(8,128)S(1)} %get-tuple-element.75), channel_id=1, source_target_pairs={{0,4},{4,8},{8,12},{12,16},{16,20},{20,24},{24,28},{28,32},{32,36}... | collective-permute-start | bytes 1179656 | tf_op jit(solution)/shard_map/ppermute | solution.py:17
  111.8 12.2 %copy-start.2 = (f32[8,192,128]{2,1,0:T(8,128)S(1)}, f32[8,192,128]{2,1,0:T(8,128)}, u32[]{:S(2)}) copy-start(f32[8,192,128]{2,1,0:T(8,128)} %copy-done.1) | copy-start | bytes 2359300
  111.8 12.2 %copy-start.48 = (f32[196608]{0:T(1024)S(1)}, f32[196608]{0:T(1024)}, u32[]{:S(2)}) copy-start(f32[196608]{0:T(1024)} %scatter_custom_fusion.4) | copy-start | bytes 2359300
  127.3 34.3 %collective-permute-start.12 = (f32[4,192,128]{2,1,0:T(8,128)}, f32[4,192,128]{2,1,0:T(8,128)}, u32[]{:S(2)}, u32[]{:S(2)}) collective-permute-start(f32[4,192,128]{2,1,0:T(8,128)} %get-tuple-element.74), channel_id=1, source_target_pairs={{4,0},{8,4},{12,8},{16,12},{20,16},{24,20},{28,24},{32,28},{36,32}... | collective-permute-start | bytes 1179656 | tf_op jit(solution)/shard_map/ppermute | solution.py:18
  129.2 32.4 %collective-permute-start.13 = (f32[4,192,128]{2,1,0:T(8,128)}, f32[4,192,128]{2,1,0:T(8,128)}, u32[]{:S(2)}, u32[]{:S(2)}) collective-permute-start(f32[4,192,128]{2,1,0:T(8,128)} %get-tuple-element.73), channel_id=1, source_target_pairs={{0,4},{4,8},{8,12},{12,16},{16,20},{20,24},{24,28},{28,32},{32,36}... | collective-permute-start | bytes 1179656 | tf_op jit(solution)/shard_map/ppermute | solution.py:17
  138.2 162.0 %collective-permute-start = (f32[4,192,128]{2,1,0:T(8,128)}, f32[4,192,128]{2,1,0:T(8,128)}, u32[]{:S(2)}, u32[]{:S(2)}) collective-permute-start(f32[4,192,128]{2,1,0:T(8,128)} %get-tuple-element.64), channel_id=1, source_target_pairs={{4,0},{8,4},{12,8},{16,12},{20,16},{24,20},{28,24},{32,28},{36,32}... | collective-permute-start | bytes 1179656 | tf_op jit(solution)/shard_map/ppermute | solution.py:18
  140.1 160.1 %collective-permute-start.1 = (f32[4,192,128]{2,1,0:T(8,128)S(1)}, f32[4,192,128]{2,1,0:T(8,128)}, u32[]{:S(2)}, u32[]{:S(2)}) collective-permute-start(f32[4,192,128]{2,1,0:T(8,128)S(1)} %get-tuple-element.63), channel_id=1, source_target_pairs={{0,4},{4,8},{8,12},{12,16},{16,20},{20,24},{24,28},{28,32},{32,36}... | collective-permute-start | bytes 1179656 | tf_op jit(solution)/shard_map/ppermute | solution.py:17
  165.0 26.7 %collective-permute-start.14 = (f32[4,192,128]{2,1,0:T(8,128)}, f32[4,192,128]{2,1,0:T(8,128)}, u32[]{:S(2)}, u32[]{:S(2)}) collective-permute-start(f32[4,192,128]{2,1,0:T(8,128)} %get-tuple-element.72), channel_id=1, source_target_pairs={{4,0},{8,4},{12,8},{16,12},{20,16},{24,20},{28,24},{32,28},{36,32}... | collective-permute-start | bytes 1179656 | tf_op jit(solution)/shard_map/ppermute | solution.py:18
  166.9 24.8 %collective-permute-start.15 = (f32[4,192,128]{2,1,0:T(8,128)}, f32[4,192,128]{2,1,0:T(8,128)}, u32[]{:S(2)}, u32[]{:S(2)}) collective-permute-start(f32[4,192,128]{2,1,0:T(8,128)} %get-tuple-element.71), channel_id=1, source_target_pairs={{0,4},{4,8},{8,12},{12,16},{16,20},{20,24},{24,28},{28,32},{32,36}... | collective-permute-start | bytes 1179656 | tf_op jit(solution)/shard_map/ppermute | solution.py:17
  195.2 24.2 %collective-permute-start.16 = (f32[4,192,128]{2,1,0:T(8,128)}, f32[4,192,128]{2,1,0:T(8,128)}, u32[]{:S(2)}, u32[]{:S(2)}) collective-permute-start(f32[4,192,128]{2,1,0:T(8,128)} %get-tuple-element.70), channel_id=1, source_target_pairs={{4,0},{8,4},{12,8},{16,12},{20,16},{24,20},{28,24},{32,28},{36,32}... | collective-permute-start | bytes 1179656 | tf_op jit(solution)/shard_map/ppermute | solution.py:18
  197.1 22.3 %collective-permute-start.17 = (f32[4,192,128]{2,1,0:T(8,128)}, f32[4,192,128]{2,1,0:T(8,128)}, u32[]{:S(2)}, u32[]{:S(2)}) collective-permute-start(f32[4,192,128]{2,1,0:T(8,128)} %get-tuple-element.69), channel_id=1, source_target_pairs={{0,4},{4,8},{8,12},{12,16},{16,20},{20,24},{24,28},{28,32},{32,36}... | collective-permute-start | bytes 1179656 | tf_op jit(solution)/shard_map/ppermute | solution.py:17
  222.8 23.9 %collective-permute-start.18 = (f32[4,192,128]{2,1,0:T(8,128)}, f32[4,192,128]{2,1,0:T(8,128)}, u32[]{:S(2)}, u32[]{:S(2)}) collective-permute-start(f32[4,192,128]{2,1,0:T(8,128)} %get-tuple-element.68), channel_id=1, source_target_pairs={{4,0},{8,4},{12,8},{16,12},{20,16},{24,20},{28,24},{32,28},{36,32}... | collective-permute-start | bytes 1179656 | tf_op jit(solution)/shard_map/ppermute | solution.py:18
  224.8 22.0 %collective-permute-start.19 = (f32[4,192,128]{2,1,0:T(8,128)}, f32[4,192,128]{2,1,0:T(8,128)}, u32[]{:S(2)}, u32[]{:S(2)}) collective-permute-start(f32[4,192,128]{2,1,0:T(8,128)} %get-tuple-element.67), channel_id=1, source_target_pairs={{0,4},{4,8},{8,12},{12,16},{16,20},{20,24},{24,28},{28,32},{32,36}... | collective-permute-start | bytes 1179656 | tf_op jit(solution)/shard_map/ppermute | solution.py:17
  250.4 32.6 %collective-permute-start.20 = (f32[4,192,128]{2,1,0:T(8,128)}, f32[4,192,128]{2,1,0:T(8,128)}, u32[]{:S(2)}, u32[]{:S(2)}) collective-permute-start(f32[4,192,128]{2,1,0:T(8,128)} %get-tuple-element.66), channel_id=1, source_target_pairs={{4,0},{8,4},{12,8},{16,12},{20,16},{24,20},{28,24},{32,28},{36,32}... | collective-permute-start | bytes 1179656 | tf_op jit(solution)/shard_map/ppermute | solution.py:18
  252.3 30.7 %collective-permute-start.21 = (f32[4,192,128]{2,1,0:T(8,128)}, f32[4,192,128]{2,1,0:T(8,128)}, u32[]{:S(2)}, u32[]{:S(2)}) collective-permute-start(f32[4,192,128]{2,1,0:T(8,128)} %get-tuple-element.65), channel_id=1, source_target_pairs={{0,4},{4,8},{8,12},{12,16},{16,20},{20,24},{24,28},{28,32},{32,36}... | collective-permute-start | bytes 1179656 | tf_op jit(solution)/shard_map/ppermute | solution.py:17
  304.1 41.0 %collective-permute-start.22 = (f32[4,192,128]{2,1,0:T(8,128)}, f32[4,192,128]{2,1,0:T(8,128)}, u32[]{:S(2)}, u32[]{:S(2)}) collective-permute-start(f32[4,192,128]{2,1,0:T(8,128)} %get-tuple-element.62), channel_id=1, source_target_pairs={{4,0},{8,4},{12,8},{16,12},{20,16},{24,20},{28,24},{32,28},{36,32}... | collective-permute-start | bytes 1179656 | tf_op jit(solution)/shard_map/ppermute | solution.py:18
  306.0 39.1 %collective-permute-start.23 = (f32[4,192,128]{2,1,0:T(8,128)S(1)}, f32[4,192,128]{2,1,0:T(8,128)}, u32[]{:S(2)}, u32[]{:S(2)}) collective-permute-start(f32[4,192,128]{2,1,0:T(8,128)S(1)} %get-tuple-element.61), channel_id=1, source_target_pairs={{0,4},{4,8},{8,12},{12,16},{16,20},{20,24},{24,28},{28,32},{32,36}... | collective-permute-start | bytes 1179656 | tf_op jit(solution)/shard_map/ppermute | solution.py:17
  349.2 26.5 %collective-permute-start.24 = (f32[4,192,128]{2,1,0:T(8,128)}, f32[4,192,128]{2,1,0:T(8,128)}, u32[]{:S(2)}, u32[]{:S(2)}) collective-permute-start(f32[4,192,128]{2,1,0:T(8,128)} %get-tuple-element.60), channel_id=1, source_target_pairs={{4,0},{8,4},{12,8},{16,12},{20,16},{24,20},{28,24},{32,28},{36,32}... | collective-permute-start | bytes 1179656 | tf_op jit(solution)/shard_map/ppermute | solution.py:18
  351.1 24.5 %collective-permute-start.25 = (f32[4,192,128]{2,1,0:T(8,128)S(1)}, f32[4,192,128]{2,1,0:T(8,128)}, u32[]{:S(2)}, u32[]{:S(2)}) collective-permute-start(f32[4,192,128]{2,1,0:T(8,128)S(1)} %get-tuple-element.59), channel_id=1, source_target_pairs={{0,4},{4,8},{8,12},{12,16},{16,20},{20,24},{24,28},{28,32},{32,36}... | collective-permute-start | bytes 1179656 | tf_op jit(solution)/shard_map/ppermute | solution.py:17
  379.2 41.0 %collective-permute-start.26 = (f32[4,192,128]{2,1,0:T(8,128)}, f32[4,192,128]{2,1,0:T(8,128)}, u32[]{:S(2)}, u32[]{:S(2)}) collective-permute-start(f32[4,192,128]{2,1,0:T(8,128)} %get-tuple-element.58), channel_id=1, source_target_pairs={{4,0},{8,4},{12,8},{16,12},{20,16},{24,20},{28,24},{32,28},{36,32}... | collective-permute-start | bytes 1179656 | tf_op jit(solution)/shard_map/ppermute | solution.py:18
  381.1 39.1 %collective-permute-start.27 = (f32[4,192,128]{2,1,0:T(8,128)S(1)}, f32[4,192,128]{2,1,0:T(8,128)}, u32[]{:S(2)}, u32[]{:S(2)}) collective-permute-start(f32[4,192,128]{2,1,0:T(8,128)S(1)} %get-tuple-element.57), channel_id=1, source_target_pairs={{0,4},{4,8},{8,12},{12,16},{16,20},{20,24},{24,28},{28,32},{32,36}... | collective-permute-start | bytes 1179656 | tf_op jit(solution)/shard_map/ppermute | solution.py:17
  423.6 27.2 %collective-permute-start.28 = (f32[4,192,128]{2,1,0:T(8,128)}, f32[4,192,128]{2,1,0:T(8,128)}, u32[]{:S(2)}, u32[]{:S(2)}) collective-permute-start(f32[4,192,128]{2,1,0:T(8,128)} %get-tuple-element.56), channel_id=1, source_target_pairs={{4,0},{8,4},{12,8},{16,12},{20,16},{24,20},{28,24},{32,28},{36,32}... | collective-permute-start | bytes 1179656 | tf_op jit(solution)/shard_map/ppermute | solution.py:18
  425.5 25.3 %collective-permute-start.29 = (f32[4,192,128]{2,1,0:T(8,128)S(1)}, f32[4,192,128]{2,1,0:T(8,128)}, u32[]{:S(2)}, u32[]{:S(2)}) collective-permute-start(f32[4,192,128]{2,1,0:T(8,128)S(1)} %get-tuple-element.55), channel_id=1, source_target_pairs={{0,4},{4,8},{8,12},{12,16},{16,20},{20,24},{24,28},{28,32},{32,36}... | collective-permute-start | bytes 1179656 | tf_op jit(solution)/shard_map/ppermute | solution.py:17
  438.6 12.1 %copy-start.25 = (f32[8,192,128]{2,1,0:T(8,128)S(1)}, f32[8,192,128]{2,1,0:T(8,128)}, u32[]{:S(2)}) copy-start(f32[8,192,128]{2,1,0:T(8,128)} %copy-done.23) | copy-start | bytes 2359300
  438.7 12.1 %copy-start.27 = (f32[8,192,128]{2,1,0:T(8,128)S(1)}, f32[8,192,128]{2,1,0:T(8,128)}, u32[]{:S(2)}) copy-start(f32[8,192,128]{2,1,0:T(8,128)} %copy-done.26) | copy-start | bytes 2359300
  454.2 37.4 %collective-permute-start.30 = (f32[4,192,128]{2,1,0:T(8,128)}, f32[4,192,128]{2,1,0:T(8,128)}, u32[]{:S(2)}, u32[]{:S(2)}) collective-permute-start(f32[4,192,128]{2,1,0:T(8,128)} %get-tuple-element.54), channel_id=1, source_target_pairs={{4,0},{8,4},{12,8},{16,12},{20,16},{24,20},{28,24},{32,28},{36,32}... | collective-permute-start | bytes 1179656 | tf_op jit(solution)/shard_map/ppermute | solution.py:18
  456.1 35.5 %collective-permute-start.31 = (f32[4,192,128]{2,1,0:T(8,128)S(1)}, f32[4,192,128]{2,1,0:T(8,128)}, u32[]{:S(2)}, u32[]{:S(2)}) collective-permute-start(f32[4,192,128]{2,1,0:T(8,128)S(1)} %get-tuple-element.53), channel_id=1, source_target_pairs={{0,4},{4,8},{8,12},{12,16},{16,20},{20,24},{24,28},{28,32},{32,36}... | collective-permute-start | bytes 1179656 | tf_op jit(solution)/shard_map/ppermute | solution.py:17
  494.9 26.2 %collective-permute-start.32 = (f32[4,192,128]{2,1,0:T(8,128)}, f32[4,192,128]{2,1,0:T(8,128)}, u32[]{:S(2)}, u32[]{:S(2)}) collective-permute-start(f32[4,192,128]{2,1,0:T(8,128)} %get-tuple-element.52), channel_id=1, source_target_pairs={{4,0},{8,4},{12,8},{16,12},{20,16},{24,20},{28,24},{32,28},{36,32}... | collective-permute-start | bytes 1179656 | tf_op jit(solution)/shard_map/ppermute | solution.py:18
  496.8 24.3 %collective-permute-start.33 = (f32[4,192,128]{2,1,0:T(8,128)S(1)}, f32[4,192,128]{2,1,0:T(8,128)}, u32[]{:S(2)}, u32[]{:S(2)}) collective-permute-start(f32[4,192,128]{2,1,0:T(8,128)S(1)} %get-tuple-element.51), channel_id=1, source_target_pairs={{0,4},{4,8},{8,12},{12,16},{16,20},{20,24},{24,28},{28,32},{32,36}... | collective-permute-start | bytes 1179656 | tf_op jit(solution)/shard_map/ppermute | solution.py:17
  524.5 32.3 %collective-permute-start.34 = (f32[4,192,128]{2,1,0:T(8,128)}, f32[4,192,128]{2,1,0:T(8,128)}, u32[]{:S(2)}, u32[]{:S(2)}) collective-permute-start(f32[4,192,128]{2,1,0:T(8,128)} %get-tuple-element.50), channel_id=1, source_target_pairs={{4,0},{8,4},{12,8},{16,12},{20,16},{24,20},{28,24},{32,28},{36,32}... | collective-permute-start | bytes 1179656 | tf_op jit(solution)/shard_map/ppermute | solution.py:18
  526.4 30.4 %collective-permute-start.35 = (f32[4,192,128]{2,1,0:T(8,128)S(1)}, f32[4,192,128]{2,1,0:T(8,128)}, u32[]{:S(2)}, u32[]{:S(2)}) collective-permute-start(f32[4,192,128]{2,1,0:T(8,128)S(1)} %get-tuple-element.49), channel_id=1, source_target_pairs={{0,4},{4,8},{8,12},{12,16},{16,20},{20,24},{24,28},{28,32},{32,36}... | collective-permute-start | bytes 1179656 | tf_op jit(solution)/shard_map/ppermute | solution.py:17
  560.3 26.1 %collective-permute-start.36 = (f32[4,192,128]{2,1,0:T(8,128)}, f32[4,192,128]{2,1,0:T(8,128)}, u32[]{:S(2)}, u32[]{:S(2)}) collective-permute-start(f32[4,192,128]{2,1,0:T(8,128)} %get-tuple-element.48), channel_id=1, source_target_pairs={{4,0},{8,4},{12,8},{16,12},{20,16},{24,20},{28,24},{32,28},{36,32}... | collective-permute-start | bytes 1179656 | tf_op jit(solution)/shard_map/ppermute | solution.py:18
  562.2 24.2 %collective-permute-start.37 = (f32[4,192,128]{2,1,0:T(8,128)S(1)}, f32[4,192,128]{2,1,0:T(8,128)}, u32[]{:S(2)}, u32[]{:S(2)}) collective-permute-start(f32[4,192,128]{2,1,0:T(8,128)S(1)} %get-tuple-element.47), channel_id=1, source_target_pairs={{0,4},{4,8},{8,12},{12,16},{16,20},{20,24},{24,28},{28,32},{32,36}... | collective-permute-start | bytes 1179656 | tf_op jit(solution)/shard_map/ppermute | solution.py:17
  589.9 26.3 %collective-permute-start.38 = (f32[4,192,128]{2,1,0:T(8,128)}, f32[4,192,128]{2,1,0:T(8,128)}, u32[]{:S(2)}, u32[]{:S(2)}) collective-permute-start(f32[4,192,128]{2,1,0:T(8,128)} %get-tuple-element.46), channel_id=1, source_target_pairs={{4,0},{8,4},{12,8},{16,12},{20,16},{24,20},{28,24},{32,28},{36,32}... | collective-permute-start | bytes 1179656 | tf_op jit(solution)/shard_map/ppermute | solution.py:18
  591.8 24.4 %collective-permute-start.39 = (f32[4,192,128]{2,1,0:T(8,128)S(1)}, f32[4,192,128]{2,1,0:T(8,128)}, u32[]{:S(2)}, u32[]{:S(2)}) collective-permute-start(f32[4,192,128]{2,1,0:T(8,128)S(1)} %get-tuple-element.45), channel_id=1, source_target_pairs={{0,4},{4,8},{8,12},{12,16},{16,20},{20,24},{24,28},{28,32},{32,36}... | collective-permute-start | bytes 1179656 | tf_op jit(solution)/shard_map/ppermute | solution.py:17
  604.4 11.8 %copy-start.8 = (f32[8,192,128]{2,1,0:T(8,128)S(1)}, f32[8,192,128]{2,1,0:T(8,128)}, u32[]{:S(2)}) copy-start(f32[8,192,128]{2,1,0:T(8,128)} %copy-done.5) | copy-start | bytes 2359300
  623.0 3.6 collective-permute-start.40
  626.7 10.3 %collective-permute-start.41 = (f32[8,48,128]{2,1,0:T(8,128)S(1)}, f32[8,48,128]{2,1,0:T(8,128)S(1)}, u32[]{:S(2)}, u32[]{:S(2)}) collective-permute-start(f32[8,48,128]{2,1,0:T(8,128)S(1)} %dynamic-slice_bitcast_fusion), channel_id=1, source_target_pairs={{0,2},{1,3},{2,0},{3,1},{4,6},{5,7},{6,4},{7,5},{8,10},{9,11},{10,... | collective-permute-start | bytes 589832 | tf_op jit(solution)/shard_map/ppermute | solution.py:160
  (60 other events, 489.8 us)
